TPU v7x, 32 devices: a whole 2x2x4 slice. The times are simulated.
32 devices in a mesh: dp: 4 (over z), section: 2 (over core), tensor: 4 (over y, x).
Axes of the slice: x: 2, y: 2, z: 4, core: 2. Of those that a mesh axis runs over, the one named last changes fastest.
Arguments:
- tokens: bfloat16 [1024, 8192], P('dp', 'tensor'), may hold values from -6 to 6
- dest_slot: int32 [1024], P('dp'), may hold values from 0 to 1023, as said below
- doc_reset: int32 [1024], P('dp'), may hold values 0 or 1
- norm_gain: float32 [2, 8192], P('section'), may hold values from 0.25 to 1.75
- w_in: bfloat16 [2, 8192, 5120], P('section', 'dp', 'tensor'), may hold values from -0.0625 to 0.0625
- w_step: bfloat16 [2, 8192, 32], P('section', None, 'tensor'), may hold values from -0.0625 to 0.0625
- step_bias: float32 [2, 32], P('section', 'tensor'), may hold values from -4 to -1.5
- a_log: float32 [2, 32], P('section', 'tensor'), may hold values from -2.5 to 1.5
- d_skip: float32 [2, 32], P('section', 'tensor'), may hold values from 0.3 to 2
- out_gain: float32 [2, 2048], P('section', 'tensor'), may hold values from 0.25 to 1.75
- w_out: bfloat16 [2, 2048, 8192], P('section', 'tensor'), may hold values from -0.125 to 0.125
Outputs:
- phase_out: bfloat16 [2, 1024, 8192], P('section', 'dp', 'tensor')
Inputs may be any that keep to these rules, and one draw needn't show every extreme that they name: dest_slot is a permutation; the tokens of one group go in order to increasing groups, and each group receives rows in order of source group. One group sends at most 128 tokens to one group, and every group sends exactly 128 to some group.
All inputs are finite; a program needn't handle non-finite values. No bound on the sum of `doc_reset` on one device may be relied on, other than what follows from the above.
Results may differ from a plain program's by a relative error of at most 0.018.
Values may be sent and summed in bfloat16 or wider, within the bound.
A program may use at most 128 MiB of HBM per device.

v0:
```python
import jax
import jax.numpy as jnp
from jax import lax
from jax.sharding import PartitionSpec as P

HEAD_DIM = 64
STATE = 128
HEADS_DEV = 8
SPAN = 64


epsilon = 1e-05


def shifted(block, axis, distance):
    devices = range(lax.axis_size(axis))
    route = [(i - distance, i) for i in devices if i - distance in devices]
    return lax.ppermute(block, axis, route)


def scan_block(inputs, writes, readout, step_size, log_decay, resets, state, skips):
    hp = lax.Precision.HIGHEST
    segment = jnp.cumsum(resets)
    cumulative = jnp.cumsum(log_decay, axis=0)
    positions = jnp.arange(resets.shape[0])
    in_segment = (segment[:, None] == segment[None, :]) & (positions[:, None] >= positions[None, :])
    gap = cumulative[:, None, :] - cumulative[None, :, :]
    decayed = jnp.where(
        in_segment[:, :, None], jnp.exp(jnp.where(in_segment[:, :, None], gap, 0.0)), 0.0
    )
    scores = jnp.einsum("thn,shn->tsh", readout, writes, precision=hp)
    weights = scores * decayed * step_size[None, :, :]
    output = jnp.einsum("tsh,shp->thp", weights, inputs, precision=hp)
    carry_ok = (segment == 0).astype(inputs.dtype)
    carried = jnp.einsum("thn,hpn->thp", readout, state, precision=hp)
    output = output + carry_ok[:, None, None] * jnp.exp(cumulative)[:, :, None] * carried
    last_seg = segment[-1]
    tail = (
        (segment == last_seg).astype(inputs.dtype)[:, None]
        * jnp.exp(cumulative[-1][None, :] - cumulative)
        * step_size
    )
    fresh = jnp.einsum("sh,shp,shn->hpn", tail, inputs, writes, precision=hp)
    kept = (last_seg == 0).astype(inputs.dtype) * jnp.exp(cumulative[-1])[:, None, None] * state
    output = output + skips[None, :, None] * inputs
    return (output, fresh + kept)


def mixer(
    full_rows, state, resets, gains, proj_w, step_w, bias_step, log_rates, skips, gains_out, out_w
):
    head_cols = HEADS_DEV * HEAD_DIM
    count = full_rows.shape[0]
    widened = full_rows.astype(jnp.float32)
    meansq = jnp.mean(widened * widened, axis=-1, keepdims=True)
    normed_in = (widened * lax.rsqrt(meansq + epsilon) * gains).astype(jnp.bfloat16)
    proj = jnp.dot(normed_in, proj_w, preferred_element_type=jnp.float32).astype(jnp.bfloat16)
    gate_proj = proj[:, :head_cols].astype(jnp.float32)
    inputs = (
        proj[:, head_cols : 2 * head_cols].astype(jnp.float32).reshape(count, HEADS_DEV, HEAD_DIM)
    )
    writes_one = proj[:, 2 * head_cols : 2 * head_cols + STATE].astype(jnp.float32)
    readout_one = proj[:, 2 * head_cols + STATE :].astype(jnp.float32)
    writes = jnp.broadcast_to(writes_one[:, None, :], (count, HEADS_DEV, STATE))
    readout = jnp.broadcast_to(readout_one[:, None, :], (count, HEADS_DEV, STATE))
    step_size = jax.nn.softplus(
        jnp.dot(normed_in, step_w, preferred_element_type=jnp.float32) + bias_step
    )
    log_decay = -jnp.exp(log_rates) * step_size
    mixed, fresh = scan_block(inputs, writes, readout, step_size, log_decay, resets, state, skips)
    gated = mixed.reshape(count, head_cols) * jax.nn.silu(gate_proj)
    meansq_out = jnp.mean(gated * gated, axis=-1, keepdims=True)
    normed = (gated * lax.rsqrt(meansq_out + epsilon) * gains_out).astype(jnp.bfloat16)
    partial_value = jnp.dot(normed, out_w, preferred_element_type=jnp.float32).astype(jnp.bfloat16)
    return (lax.optimization_barrier(partial_value).astype(jnp.float32), fresh)


def per_device(
    tokens, dest_slot, doc_reset, norm_gain, w_in, w_step, step_bias, a_log, d_skip, out_gain, w_out
):
    groups = lax.axis_size("dp")
    row_count = tokens.shape[0]
    feat_local = tokens.shape[1]
    capacity = 2 * row_count // groups
    target = dest_slot // row_count
    onehot = (target[:, None] == jnp.arange(groups)[None, :]).astype(jnp.int32)
    before = jnp.cumsum(onehot, axis=0) - onehot
    placed = jnp.sum(onehot * before, axis=1)
    slots = target * capacity + placed
    outbox = jnp.zeros((groups * capacity, feat_local), jnp.bfloat16).at[slots].set(tokens)
    marks = (
        jnp.full((groups * capacity,), row_count, jnp.int32).at[slots].set(dest_slot % row_count)
    )
    inbox, where_to = (
        lax.all_to_all(
            outbox.reshape(groups, capacity, feat_local),
            "dp",
            split_axis=0,
            concat_axis=0,
            tiled=True,
        ),
        lax.all_to_all(
            marks.reshape(groups, capacity), "dp", split_axis=0, concat_axis=0, tiled=True
        ),
    )
    balanced = (
        jnp.zeros((row_count, feat_local), jnp.bfloat16)
        .at[where_to.reshape(-1)]
        .set(inbox.reshape(-1, feat_local), mode="drop")
    )
    gains = norm_gain[0]
    proj_w = lax.all_gather(w_in[0], "dp", axis=0, tiled=True)
    step_w = w_step[0]
    bias_step = step_bias[0]
    log_rates = a_log[0]
    skips = d_skip[0]
    gains_out = out_gain[0]
    out_w = w_out[0]
    phases = lax.axis_size("section")
    phase_idx = lax.axis_index("section")
    blocks = row_count // SPAN
    source = balanced
    source = source.reshape(blocks, SPAN, source.shape[1])
    resets_all = doc_reset.reshape(blocks, SPAN)
    state = jnp.zeros((HEADS_DEV, HEAD_DIM, STATE), jnp.float32)
    results = jnp.zeros((blocks, SPAN, feat_local), jnp.bfloat16)
    incoming = jnp.zeros_like(source[0])
    for clock_tick in range(blocks + phases - 1):
        micro = clock_tick - phase_idx
        active = (micro >= 0) & (micro < blocks)
        picked = jnp.clip(micro, 0, blocks - 1)
        first_in = lax.dynamic_index_in_dim(source, picked, 0, keepdims=False)
        hin = jnp.where(phase_idx == 0, first_in, incoming)
        resets = lax.dynamic_index_in_dim(resets_all, picked, 0, keepdims=False)
        full_rows = lax.all_gather(hin, "tensor", axis=1, tiled=True)
        partial_value, fresh = mixer(
            full_rows,
            state,
            resets,
            gains,
            proj_w,
            step_w,
            bias_step,
            log_rates,
            skips,
            gains_out,
            out_w,
        )
        summed = lax.psum_scatter(
            partial_value.astype(jnp.bfloat16), "tensor", scatter_dimension=1, tiled=True
        ).astype(jnp.float32)
        hout = (hin.astype(jnp.float32) + summed).astype(jnp.bfloat16)
        state = jnp.where(active, fresh, state)
        updated = lax.dynamic_update_index_in_dim(results, hout, picked, 0)
        results = jnp.where(active, updated, results)
        incoming = shifted(hout, "section", 1)
    return results.reshape(1, row_count, feat_local)


def solution(mesh):
    placed = (
        P("dp", "tensor"),
        P("dp"),
        P("dp"),
        P("section", None),
        P("section", "dp", "tensor"),
        P("section", None, "tensor"),
        P("section", "tensor"),
        P("section", "tensor"),
        P("section", "tensor"),
        P("section", "tensor"),
        P("section", "tensor", None),
    )
    return jax.shard_map(
        per_device,
        mesh=mesh,
        in_specs=placed,
        out_specs=P("section", "dp", "tensor"),
        check_vma=False,
    )
```

profile of v0, /device:TPU:0, one launch (start us, length us, event | category | flops | bytes accessed | tf_op | source)
XLA Modules:
  0.0 839.3 jit_solution(8182304182373492023)
XLA Ops:
  7.3 1.2 reduce-window.21
  8.9 2.0 scatter_custom_fusion
  10.9 6.3 all-to-all-start
  17.2 4.4 scatter_custom_fusion.1
  21.7 1.1 all-to-all-done
  22.7 4.0 all-to-all-start.1
  26.8 47.6 %all-to-all-done.1 = bf16[4,128,2048]{2,1,0:T(8,128)(2,1)S(1)} async-done(((bf16[4,128,2048]{2,1,0:T(8,128)(2,1)}), bf16[4,128,2048]{2,1,0:T(8,128)(2,1)S(1)}, u32[]{:S(2)}, u32[]{:S(2)}) %all-to-all-start.1) | async-done | bytes 2097184 | tf_op jit(solution)/shard_map/all_to_all | solution.py:95
  74.4 3.8 scatter_custom_fusion.2
  82.2 22.5 %all-gather.17.cloned.1.call-done = bf16[1,64,8192]{2,1,0:T(8,128)(2,1)} async-done(((bf16[1,64,2048]{2,1,0:T(8,128)(2,1)}), bf16[1,64,8192]{2,1,0:T(8,128)(2,1)}) %all-gather.17.cloned.1.call-update) | async-done | bytes 1048592 | tf_op jit(solution)/shard_map/all_gather | solution.py:135
  104.7 1.6 fusion.42
  106.3 1.7 broadcast_multiply_fusion.4
  108.4 354.7 %all-gather.19.cloned.1.call-done = bf16[1,8192,1280]{2,1,0:T(8,128)(2,1)} async-done(((bf16[1,2048,1280]{2,1,0:T(8,128)(2,1)}), bf16[1,8192,1280]{2,1,0:T(8,128)(2,1)}) %all-gather.19.cloned.1.call-update) | async-done | bytes 20971536 | tf_op jit(solution)/shard_map/all_gather | solution.py:112
  463.1 9.0 %fusion.15 = bf16[64,1280]{1,0:T(8,128)(2,1)S(1)} fusion(bf16[1,8192,1280]{2,1,0:T(8,128)(2,1)} %all-gather.19.cloned.1.call-done, bf16[1,64,8192]{2,1,0:T(8,128)(2,1)S(1)} %copy-done.1, f32[8192]{0:T(1024)S(1)} %bitcast.280, f32[64]{0:T(128)S(1)} %add_rsqrt_fusion.9), kind=kOutput, calls=%fused_computation.33 | convolution fusion | flops 1344356352 | bytes 22216960 | tf_op jit(solution)/shard_map/dot_general | solution.py:57
  474.0 6.0 convolution_convert_fusion.4
  480.1 26.6 %reduce-scatter.6.cloned.1.call-done = bf16[64,2048]{1,0:T(8,128)(2,1)} async-done(((bf16[64,8192]{1,0:T(8,128)(2,1)}), bf16[64,2048]{1,0:T(8,128)(2,1)}) %reduce-scatter.6.cloned.1.call-update) | async-done | bytes 262160 | tf_op jit(solution)/shard_map/reduce_scatter | solution.py:149
  507.9 1.6 collective-permute-start
  509.5 1.1 collective-permute-done
  512.9 1.2 compare_convert_fusion.5
  514.7 23.4 %all-gather.9.cloned.1.call-done = bf16[64,8192]{1,0:T(8,128)(2,1)} async-done(((bf16[64,2048]{1,0:T(8,128)(2,1)}), bf16[64,8192]{1,0:T(8,128)(2,1)}) %all-gather.9.cloned.1.call-update) | async-done | bytes 1048592 | tf_op jit(solution)/shard_map/all_gather | solution.py:135
  538.0 1.5 fusion.30
  539.6 11.1 %fusion.18 = bf16[64,1280]{1,0:T(8,128)(2,1)S(1)} fusion(bf16[1,8192,1280]{2,1,0:T(8,128)(2,1)} %all-gather.19.cloned.1.call-done, bf16[64,8192]{1,0:T(8,128)(2,1)} %all-gather.9.cloned.1.call-done, f32[64]{0:T(128)S(1)} %add_rsqrt_fusion.7, f32[8192]{0:T(1024)S(1)} %bitcast.281), kind=kOutput, calls=%fused_computation.34 | convolution fusion | flops 1344356352 | bytes 22216960 | tf_op jit(solution)/shard_map/dot_general | solution.py:57
  553.5 6.0 convolution_convert_fusion.3
  559.6 28.0 %reduce-scatter.8.cloned.1.call-done = bf16[64,2048]{1,0:T(8,128)(2,1)} async-done(((bf16[64,8192]{1,0:T(8,128)(2,1)}), bf16[64,2048]{1,0:T(8,128)(2,1)}) %reduce-scatter.8.cloned.1.call-update) | async-done | bytes 262160 | tf_op jit(solution)/shard_map/reduce_scatter | solution.py:149
  587.7 1.1 fusion.94
  588.8 1.6 collective-permute-start.1
  590.3 1.1 collective-permute-done.1
  594.4 1.2 compare_convert_fusion.3
  596.8 22.1 %all-gather.11.cloned.1.call-done = bf16[64,8192]{1,0:T(8,128)(2,1)} async-done(((bf16[64,2048]{1,0:T(8,128)(2,1)}), bf16[64,8192]{1,0:T(8,128)(2,1)}) %all-gather.11.cloned.1.call-update) | async-done | bytes 1048592 | tf_op jit(solution)/shard_map/all_gather | solution.py:135
  619.0 1.5 fusion.33
  620.5 11.1 %fusion.21 = bf16[64,1280]{1,0:T(8,128)(2,1)S(1)} fusion(bf16[1,8192,1280]{2,1,0:T(8,128)(2,1)} %all-gather.19.cloned.1.call-done, bf16[64,8192]{1,0:T(8,128)(2,1)} %all-gather.11.cloned.1.call-done, f32[64]{0:T(128)S(1)} %add_rsqrt_fusion.5, f32[8192]{0:T(1024)S(1)} %bitcast.283), kind=kOutput, calls=%fused_computation.35 | convolution fusion | flops 1344356352 | bytes 22216960 | tf_op jit(solution)/shard_map/dot_general | solution.py:57
  634.5 6.0 convolution_convert_fusion.2
  640.6 28.0 %reduce-scatter.10.cloned.1.call-done = bf16[64,2048]{1,0:T(8,128)(2,1)} async-done(((bf16[64,8192]{1,0:T(8,128)(2,1)}), bf16[64,2048]{1,0:T(8,128)(2,1)}) %reduce-scatter.10.cloned.1.call-update) | async-done | bytes 262160 | tf_op jit(solution)/shard_map/reduce_scatter | solution.py:149
  668.6 1.1 fusion.93
  669.7 1.6 collective-permute-start.2
  671.3 1.1 collective-permute-done.2
  675.0 1.1 compare_convert_fusion.1
  677.3 22.6 %all-gather.13.cloned.1.call-done = bf16[64,8192]{1,0:T(8,128)(2,1)} async-done(((bf16[64,2048]{1,0:T(8,128)(2,1)}), bf16[64,8192]{1,0:T(8,128)(2,1)}) %all-gather.13.cloned.1.call-update) | async-done | bytes 1048592 | tf_op jit(solution)/shard_map/all_gather | solution.py:135
  699.9 1.5 fusion.36
  701.5 11.1 %fusion.24 = bf16[64,1280]{1,0:T(8,128)(2,1)S(1)} fusion(bf16[1,8192,1280]{2,1,0:T(8,128)(2,1)} %all-gather.19.cloned.1.call-done, bf16[64,8192]{1,0:T(8,128)(2,1)} %all-gather.13.cloned.1.call-done, f32[64]{0:T(128)S(1)} %add_rsqrt_fusion.3, f32[8192]{0:T(1024)S(1)} %bitcast.285), kind=kOutput, calls=%fused_computation.36 | convolution fusion | flops 1344356352 | bytes 22216960 | tf_op jit(solution)/shard_map/dot_general | solution.py:57
  715.4 6.0 convolution_convert_fusion.1
  721.5 28.0 %reduce-scatter.12.cloned.1.call-done = bf16[64,2048]{1,0:T(8,128)(2,1)} async-done(((bf16[64,8192]{1,0:T(8,128)(2,1)}), bf16[64,2048]{1,0:T(8,128)(2,1)}) %reduce-scatter.12.cloned.1.call-update) | async-done | bytes 262160 | tf_op jit(solution)/shard_map/reduce_scatter | solution.py:149
  750.6 1.6 collective-permute-start.3
  752.2 1.1 collective-permute-done.3
  755.9 24.9 %all-gather.15.cloned.1.call-done = bf16[64,8192]{1,0:T(8,128)(2,1)} async-done(((bf16[64,2048]{1,0:T(8,128)(2,1)}), bf16[64,8192]{1,0:T(8,128)(2,1)}) %all-gather.15.cloned.1.call-update) | async-done | bytes 1048592 | tf_op jit(solution)/shard_map/all_gather | solution.py:135
  780.8 1.5 fusion.39
  782.4 11.1 %fusion.27 = bf16[64,1280]{1,0:T(8,128)(2,1)S(1)} fusion(bf16[1,8192,1280]{2,1,0:T(8,128)(2,1)} %all-gather.19.cloned.1.call-done, bf16[64,8192]{1,0:T(8,128)(2,1)} %all-gather.15.cloned.1.call-done, f32[64]{0:T(128)S(1)} %add_rsqrt_fusion.1, f32[8192]{0:T(1024)S(1)} %bitcast.287), kind=kOutput, calls=%fused_computation.37 | convolution fusion | flops 1344356352 | bytes 22216960 | tf_op jit(solution)/shard_map/dot_general | solution.py:57
  796.3 6.0 convolution_convert_fusion
  802.4 28.1 %reduce-scatter.14.cloned.1.call-done = bf16[64,2048]{1,0:T(8,128)(2,1)} async-done(((bf16[64,8192]{1,0:T(8,128)(2,1)}), bf16[64,2048]{1,0:T(8,128)(2,1)}) %reduce-scatter.14.cloned.1.call-update) | async-done | bytes 262160 | tf_op jit(solution)/shard_map/reduce_scatter | solution.py:149
  (230 shorter events, 33.3 us)
Async XLA Ops:
  6.5 99.8 %copy-start = (bf16[1,8192,8]{1,2,0:T(8,128)(2,1)S(1)}, bf16[1,8192,8]{1,2,0:T(8,128)(2,1)}, u32[]{:S(2)}) copy-start(bf16[1,8192,8]{1,2,0:T(8,128)(2,1)} %param.16) | copy-start | bytes 393220
  10.9 11.8 %all-to-all-start = ((s32[4,1,128]{2,1,0:T(1,128)}), s32[4,1,128]{2,1,0:T(1,128)S(1)}, u32[]{:S(2)}, u32[]{:S(2)}) async-start(s32[4,1,128]{2,1,0:T(1,128)} %bitcast.3), calls=%async_computation | async-start | bytes 4096 | tf_op jit(solution)/shard_map/all_to_all | solution.py:102
  22.7 51.7 %all-to-all-start.1 = ((bf16[4,128,2048]{2,1,0:T(8,128)(2,1)}), bf16[4,128,2048]{2,1,0:T(8,128)(2,1)S(1)}, u32[]{:S(2)}, u32[]{:S(2)}) async-start(bf16[4,128,2048]{2,1,0:T(8,128)(2,1)} %bitcast.6), calls=%async_computation.1 | async-start | bytes 4194304 | tf_op jit(solution)/shard_map/all_to_all | solution.py:95
  26.7 77.9 %all-gather.17.cloned.1.call-start = ((), (), s32[]{:S(2)}) async-start(), calls=%async_computation.16 | async-start | bytes 1310720 | tf_op jit(solution)/shard_map/all_gather | solution.py:135
  78.9 1.2 copy-start.22
  78.9 2.6 copy-start.23
  78.9 27.4 %copy-start.7 = (f32[1,8192]{1,0:T(1,128)S(1)}, f32[1,8192]{1,0:T(1,128)}, u32[]{:S(2)}) copy-start(f32[1,8192]{1,0:T(1,128)} %param.14) | copy-start | bytes 98308
  79.0 27.4 %copy-start.24 = (f32[1,8]{1,0:T(1,128)S(1)}, f32[1,8]{1,0:T(1,128)}, u32[]{:S(2)}) copy-start(f32[1,8]{1,0:T(1,128)} %param.17) | copy-start | bytes 100
  79.0 384.1 %all-gather.19.cloned.1.call-start = ((), (), s32[]{:S(2)}) async-start(), calls=%async_computation.17 | async-start | bytes 26214400 | tf_op jit(solution)/shard_map/all_gather | solution.py:112
  79.7 427.0 %reduce-scatter.6.cloned.1.call-start = ((), (), s32[]{:S(2)}) async-start(), calls=%async_computation.7 | async-start | bytes 1310720 | tf_op jit(solution)/shard_map/reduce_scatter | solution.py:149
  81.6 469.2 %copy-start.28 = (f32[8]{0:T(128)}, f32[8]{0:T(128)S(1)}, u32[]{:S(2)}) copy-start(f32[8]{0:T(128)S(1)} %negate_bitcast_fusion) | copy-start | bytes 100
  104.7 358.4 %copy-start.1 = (bf16[1,64,8192]{2,1,0:T(8,128)(2,1)S(1)}, bf16[1,64,8192]{2,1,0:T(8,128)(2,1)}, u32[]{:S(2)}) copy-start(bf16[1,64,8192]{2,1,0:T(8,128)(2,1)} %all-gather.17.cloned.1.call-done) | copy-start | bytes 3145732
  108.4 364.7 %copy-start.13 = (f32[1,8]{1,0:T(1,128)S(1)}, f32[1,8]{1,0:T(1,128)}, u32[]{:S(2)}) copy-start(f32[1,8]{1,0:T(1,128)} %param.19) | copy-start | bytes 100
  472.1 1.9 copy-start.12
  480.0 58.0 %all-gather.9.cloned.1.call-start = ((), (), s32[]{:S(2)}) async-start(), calls=%async_computation.8 | async-start | bytes 1310720 | tf_op jit(solution)/shard_map/all_gather | solution.py:135
  507.9 2.7 collective-permute-start
  511.4 76.3 %reduce-scatter.8.cloned.1.call-start = ((), (), s32[]{:S(2)}) async-start(), calls=%async_computation.9 | async-start | bytes 1310720 | tf_op jit(solution)/shard_map/reduce_scatter | solution.py:149
  539.6 11.2 %copy-start.5 = (bf16[64,8192]{1,0:T(8,128)(2,1)S(1)}, bf16[64,8192]{1,0:T(8,128)(2,1)}, u32[]{:S(2)}) copy-start(bf16[64,8192]{1,0:T(8,128)(2,1)} %all-gather.9.cloned.1.call-done) | copy-start | bytes 3145732
  553.5 34.1 %copy-start.11 = (bf16[64,2048]{1,0:T(8,128)(2,1)S(1)}, bf16[64,2048]{1,0:T(8,128)(2,1)}, u32[]{:S(2)}) copy-start(bf16[64,2048]{1,0:T(8,128)(2,1)} %bitcast_select_fusion.6) | copy-start | bytes 786436
  559.6 33.9 %copy-start.18 = (s32[64,1]{0,1:T(1,128)S(1)}, s32[64,1]{0,1:T(1,128)}, u32[]{:S(2)}) copy-start(s32[64,1]{0,1:T(1,128)} %get-tuple-element.25) | copy-start | bytes 772
  559.6 36.8 %copy-start.21 = (f32[64]{0:T(128)S(1)}, f32[64]{0:T(128)}, u32[]{:S(2)}) copy-start(f32[64]{0:T(128)} %get-tuple-element.34) | copy-start | bytes 772
  559.6 59.4 %all-gather.11.cloned.1.call-start = ((), (), s32[]{:S(2)}) async-start(), calls=%async_computation.10 | async-start | bytes 1310720 | tf_op jit(solution)/shard_map/all_gather | solution.py:135
  588.8 2.7 collective-permute-start.1
  592.2 76.4 %reduce-scatter.10.cloned.1.call-start = ((), (), s32[]{:S(2)}) async-start(), calls=%async_computation.11 | async-start | bytes 1310720 | tf_op jit(solution)/shard_map/reduce_scatter | solution.py:149
  620.5 11.2 %copy-start.2 = (bf16[64,8192]{1,0:T(8,128)(2,1)S(1)}, bf16[64,8192]{1,0:T(8,128)(2,1)}, u32[]{:S(2)}) copy-start(bf16[64,8192]{1,0:T(8,128)(2,1)} %all-gather.11.cloned.1.call-done) | copy-start | bytes 3145732
  620.5 11.2 %copy-start.25 = (f32[1,8]{1,0:T(1,128)S(1)}, f32[1,8]{1,0:T(1,128)}, u32[]{:S(2)}) copy-start(f32[1,8]{1,0:T(1,128)} %param.17) | copy-start | bytes 100
  620.5 11.2 %copy-start.29 = (f32[8]{0:T(128)S(1)}, f32[8]{0:T(128)}, u32[]{:S(2)}) copy-start(f32[8]{0:T(128)} %copy-done.28) | copy-start | bytes 100
  631.7 1.1 copy-start.14
  634.5 34.1 %copy-start.9 = (bf16[64,2048]{1,0:T(8,128)(2,1)S(1)}, bf16[64,2048]{1,0:T(8,128)(2,1)}, u32[]{:S(2)}) copy-start(bf16[64,2048]{1,0:T(8,128)(2,1)} %bitcast_select_fusion.4) | copy-start | bytes 786436
  640.5 32.9 %copy-start.17 = (s32[64,1]{0,1:T(1,128)S(1)}, s32[64,1]{0,1:T(1,128)}, u32[]{:S(2)}) copy-start(s32[64,1]{0,1:T(1,128)} %get-tuple-element.24) | copy-start | bytes 772
  640.5 36.3 %copy-start.19 = (f32[64]{0:T(128)S(1)}, f32[64]{0:T(128)}, u32[]{:S(2)}) copy-start(f32[64]{0:T(128)} %get-tuple-element.32) | copy-start | bytes 772
  640.6 59.3 %all-gather.13.cloned.1.call-start = ((), (), s32[]{:S(2)}) async-start(), calls=%async_computation.12 | async-start | bytes 1310720 | tf_op jit(solution)/shard_map/all_gather | solution.py:135
  669.7 2.7 collective-permute-start.2
  673.2 76.4 %reduce-scatter.12.cloned.1.call-start = ((), (), s32[]{:S(2)}) async-start(), calls=%async_computation.13 | async-start | bytes 1310720 | tf_op jit(solution)/shard_map/reduce_scatter | solution.py:149
  701.4 11.2 %copy-start.3 = (bf16[64,8192]{1,0:T(8,128)(2,1)S(1)}, bf16[64,8192]{1,0:T(8,128)(2,1)}, u32[]{:S(2)}) copy-start(bf16[64,8192]{1,0:T(8,128)(2,1)} %all-gather.13.cloned.1.call-done) | copy-start | bytes 3145732
  701.4 11.2 %copy-start.26 = (f32[1,8]{1,0:T(1,128)S(1)}, f32[1,8]{1,0:T(1,128)}, u32[]{:S(2)}) copy-start(f32[1,8]{1,0:T(1,128)} %param.17) | copy-start | bytes 100
  701.4 11.2 %copy-start.30 = (f32[8]{0:T(128)S(1)}, f32[8]{0:T(128)}, u32[]{:S(2)}) copy-start(f32[8]{0:T(128)} %copy-done.28) | copy-start | bytes 100
  712.6 1.1 copy-start.15
  715.4 34.1 %copy-start.10 = (bf16[64,2048]{1,0:T(8,128)(2,1)S(1)}, bf16[64,2048]{1,0:T(8,128)(2,1)}, u32[]{:S(2)}) copy-start(bf16[64,2048]{1,0:T(8,128)(2,1)} %bitcast_select_fusion.2) | copy-start | bytes 786436
  721.4 33.6 %copy-start.16 = (s32[64,1]{0,1:T(1,128)S(1)}, s32[64,1]{0,1:T(1,128)}, u32[]{:S(2)}) copy-start(s32[64,1]{0,1:T(1,128)} %get-tuple-element.23) | copy-start | bytes 772
  721.4 34.0 %copy-start.20 = (f32[64]{0:T(128)S(1)}, f32[64]{0:T(128)}, u32[]{:S(2)}) copy-start(f32[64]{0:T(128)} %get-tuple-element.30) | copy-start | bytes 772
  721.5 59.3 %all-gather.15.cloned.1.call-start = ((), (), s32[]{:S(2)}) async-start(), calls=%async_computation.14 | async-start | bytes 1310720 | tf_op jit(solution)/shard_map/all_gather | solution.py:135
  750.6 2.7 collective-permute-start.3
  754.1 76.3 %reduce-scatter.14.cloned.1.call-start = ((), (), s32[]{:S(2)}) async-start(), calls=%async_computation.15 | async-start | bytes 1310720 | tf_op jit(solution)/shard_map/reduce_scatter | solution.py:149
  782.3 11.2 %copy-start.4 = (bf16[64,8192]{1,0:T(8,128)(2,1)S(1)}, bf16[64,8192]{1,0:T(8,128)(2,1)}, u32[]{:S(2)}) copy-start(bf16[64,8192]{1,0:T(8,128)(2,1)} %all-gather.15.cloned.1.call-done) | copy-start | bytes 3145732
  782.4 11.2 %copy-start.27 = (f32[1,8]{1,0:T(1,128)S(1)}, f32[1,8]{1,0:T(1,128)}, u32[]{:S(2)}) copy-start(f32[1,8]{1,0:T(1,128)} %param.17) | copy-start | bytes 100
  782.4 11.2 %copy-start.31 = (f32[8]{0:T(128)S(1)}, f32[8]{0:T(128)}, u32[]{:S(2)}) copy-start(f32[8]{0:T(128)} %copy-done.28) | copy-start | bytes 100
  796.3 34.1 %copy-start.8 = (bf16[64,2048]{1,0:T(8,128)(2,1)S(1)}, bf16[64,2048]{1,0:T(8,128)(2,1)}, u32[]{:S(2)}) copy-start(bf16[64,2048]{1,0:T(8,128)(2,1)} %bitcast_select_fusion) | copy-start | bytes 786436
  (1 other events, 1.0 us)
Sparse Core Ops, SparseCore 0:
  79.0 25.5 all-gather.16
  106.3 356.8 all-gather.18
  480.1 26.4 reduce-scatter.5
  511.5 26.4 all-gather.8
  559.7 27.9 reduce-scatter.7
  592.4 26.5 all-gather.10
  640.7 27.9 reduce-scatter.9
  673.3 26.5 all-gather.12
  721.6 27.9 reduce-scatter.11
  754.2 26.5 all-gather.14
  802.5 27.9 reduce-scatter.13
where the time goes:
time: 846 us; the launch traced here: 839 us
  waiting for transfers between devices  663 us (78%)
  matrix products  95.9 us (11%)
  other arithmetic  27.7 us (3%)
  starting transfers between devices  18.4 us (2%)
  local copies, waits for them, and re-layouts  17.3 us (2%)
  between operations  17.1 us (2%)
    all_gather x1, waiting for transfers between devices, per_device(): proj_w = lax.all_gather(w_in[0], 'dp', axis=0, tiled=True)  355 us
    reduce_scatter x5, waiting for transfers between devices, per_device(): lax.psum_scatter(partial_value.astype(jnp.bfloat16), 'tensor', scatter_di...  139 us
    all_gather x5, waiting for transfers between devices, per_device(): full_rows = lax.all_gather(hin, 'tensor', axis=1, tiled=True)  115 us
    dot_general x5, matrix products, mixer(): jnp.dot(normed_in, proj_w, preferred_element_type=jnp.float32)  53.5 us
    all_to_all x1, waiting for transfers between devices, per_device(): lax.all_to_all(outbox.reshape(groups, capacity, feat_local), 'dp', split_...  47.6 us
    dot_general x5, matrix products, mixer(): jnp.dot(normed, out_w, preferred_element_type=jnp.float32)  30.1 us
  transfers between devices with their start and end apart: 17, of which 17 were waited for; matrix products, arithmetic and copies ran while one was open for 2% of the time, Pallas kernels for 0%

commit v1 on v0

v1 whole, which is shorter than its diff:
```python
import jax
import jax.numpy as jnp
from jax import lax
from jax.sharding import PartitionSpec as P

HEAD_DIM = 64
STATE = 128
HEADS_DEV = 8
SPAN = 64


epsilon = 1e-05


def scan_block(inputs, writes, readout, step_size, log_decay, resets, state, skips):
    segment = jnp.cumsum(resets)
    cumulative = jnp.cumsum(log_decay, axis=0)
    positions = jnp.arange(resets.shape[0])
    in_segment = (segment[:, None] == segment[None, :]) & (positions[:, None] >= positions[None, :])
    by_head = cumulative.T
    gap = by_head[:, :, None] - by_head[:, None, :]
    decayed = jnp.where(in_segment[None], jnp.exp(jnp.where(in_segment[None], gap, 0.0)), 0.0)
    f32 = jnp.float32
    scores = jnp.einsum("tn,sn->ts", readout, writes, preferred_element_type=f32)
    weights = scores[None] * decayed * step_size.T[:, None, :]
    output = jnp.einsum("hts,shp->thp", weights, inputs.astype(f32))
    carry_ok = (segment == 0).astype(f32)
    carried = jnp.einsum("tn,hpn->thp", readout.astype(f32), state)
    output = output + carry_ok[:, None, None] * jnp.exp(cumulative)[:, :, None] * carried
    last_seg = segment[-1]
    tail = (
        (segment == last_seg).astype(f32)[:, None]
        * jnp.exp(cumulative[-1][None, :] - cumulative)
        * step_size
    )
    fresh = jnp.einsum("shp,sn->hpn", tail[:, :, None] * inputs.astype(f32), writes.astype(f32))
    kept = (last_seg == 0).astype(f32) * jnp.exp(cumulative[-1])[:, None, None] * state
    output = output + skips[None, :, None] * inputs.astype(f32)
    return (output, fresh + kept)


def per_device(
    tokens, dest_slot, doc_reset, norm_gain, w_in, w_step, step_bias, a_log, d_skip, out_gain, w_out
):
    f32, bf16 = jnp.float32, jnp.bfloat16
    groups = lax.axis_size("dp")
    width = lax.axis_size("tensor")
    cores = lax.axis_size("section")
    layers = cores
    dp_idx = lax.axis_index("dp")
    core = lax.axis_index("section")
    row_count = tokens.shape[0]
    feat_local = tokens.shape[1]
    feats = feat_local * width
    capacity = 2 * row_count // groups
    head_cols = HEADS_DEV * HEAD_DIM

    def whole(param):
        return lax.all_gather(param, "section", axis=0, tiled=True)

    w_in, w_out, w_step = whole(w_in), whole(w_out), whole(w_step)
    norm_gain, step_bias, a_log, d_skip, out_gain = (
        whole(norm_gain), whole(step_bias), whole(a_log), whole(d_skip), whole(out_gain)
    )

    part = feat_local // cores
    mine = lax.dynamic_slice_in_dim(tokens, core * part, part, axis=1)
    target = dest_slot // row_count
    onehot = (target[:, None] == jnp.arange(groups)[None, :]).astype(jnp.int32)
    before = jnp.cumsum(onehot, axis=0) - onehot
    placed = jnp.sum(onehot * before, axis=1)
    slots = target * capacity + placed
    outbox = jnp.zeros((groups * capacity, part), bf16).at[slots].set(mine)
    marks = (
        jnp.full((groups * capacity,), row_count, jnp.int32).at[slots].set(dest_slot % row_count)
    )
    inbox = lax.all_to_all(
        outbox.reshape(groups, capacity, part), "dp", split_axis=0, concat_axis=0, tiled=True
    )
    where_to = lax.all_to_all(
        marks.reshape(groups, capacity), "dp", split_axis=0, concat_axis=0, tiled=True
    )
    balanced = (
        jnp.zeros((row_count, part), bf16)
        .at[where_to.reshape(-1)]
        .set(inbox.reshape(-1, part), mode="drop")
    )
    few = row_count // (cores * width)
    half = row_count // cores
    rows = lax.all_to_all(
        balanced.reshape(cores * width, few, part), ("section", "tensor"), 0, 0, tiled=True
    )
    rows = rows.reshape(cores, width, few, part).transpose(2, 1, 0, 3).reshape(few, feats)

    depth = w_in.shape[1]
    outs = []
    for layer in range(layers):
        widened = rows.astype(f32)
        meansq = jnp.mean(widened * widened, axis=-1, keepdims=True)
        u = (widened * lax.rsqrt(meansq + epsilon) * norm_gain[layer]).astype(bf16)
        u = u.reshape(few, groups, depth).transpose(1, 0, 2)
        u = lax.all_to_all(u, "dp", 0, 0, tiled=True)
        step_w = lax.dynamic_slice_in_dim(w_step[layer], dp_idx * depth, depth, axis=0)
        full_u = lax.all_gather(u, "tensor", axis=1, tiled=True)
        full_u = full_u.reshape(groups * half, depth)
        proj = jnp.dot(full_u, w_in[layer], preferred_element_type=f32).astype(bf16)
        pre = jnp.dot(full_u, step_w, preferred_element_type=f32)
        proj = lax.all_to_all(proj.reshape(groups, half, -1), "dp", 0, 0, tiled=True)
        pre = lax.all_to_all(pre.reshape(groups, half, HEADS_DEV), "dp", 0, 0, tiled=True)
        proj = jnp.sum(proj.astype(f32), axis=0).astype(bf16)
        pre = jnp.sum(pre, axis=0)
        proj = lax.all_gather(proj, "section", axis=0, tiled=True)
        pre = lax.all_gather(pre, "section", axis=0, tiled=True)
        step_size = jax.nn.softplus(pre + step_bias[layer])
        log_decay = -jnp.exp(a_log[layer]) * step_size
        state = jnp.zeros((HEADS_DEV, HEAD_DIM, STATE), f32)
        mixed = []
        for at in range(0, row_count, SPAN):
            span = slice(at, at + SPAN)
            output, state = scan_block(
                proj[span, head_cols : 2 * head_cols].reshape(SPAN, HEADS_DEV, HEAD_DIM),
                proj[span, 2 * head_cols : 2 * head_cols + STATE],
                proj[span, 2 * head_cols + STATE :],
                step_size[span],
                log_decay[span],
                doc_reset[span],
                state,
                d_skip[layer],
            )
            mixed.append(output.reshape(SPAN, head_cols))
        mixed = jnp.concatenate(mixed, axis=0)
        mixed = lax.dynamic_slice_in_dim(mixed, core * half, half, axis=0)
        gate = lax.dynamic_slice_in_dim(proj[:, :head_cols], core * half, half, axis=0).astype(f32)
        gated = mixed * jax.nn.silu(gate)
        meansq_out = jnp.mean(gated * gated, axis=-1, keepdims=True)
        normed = (gated * lax.rsqrt(meansq_out + epsilon) * out_gain[layer]).astype(bf16)
        partial_value = jnp.dot(normed, w_out[layer], preferred_element_type=f32).astype(bf16)
        partial_value = lax.all_to_all(
            partial_value.reshape(width, few, feats), "tensor", 0, 0, tiled=True
        )
        summed = jnp.sum(partial_value.astype(f32), axis=0)
        rows = (widened + summed).astype(bf16)
        outs.append(rows.reshape(few, width, feat_local).transpose(1, 0, 2))
    outs = jnp.concatenate(outs, axis=0)
    outs = lax.all_to_all(outs, ("section", "tensor"), 0, 0, tiled=True)
    return outs.reshape(1, row_count, feat_local)


def solution(mesh):
    placed = (
        P("dp", "tensor"),
        P("dp"),
        P("dp"),
        P("section", None),
        P("section", "dp", "tensor"),
        P("section", None, "tensor"),
        P("section", "tensor"),
        P("section", "tensor"),
        P("section", "tensor"),
        P("section", "tensor"),
        P("section", "tensor", None),
    )
    return jax.shard_map(
        per_device,
        mesh=mesh,
        in_specs=placed,
        out_specs=P("section", "dp", "tensor"),
        check_vma=False,
    )
```

time: 846 us -> 415 us (0.49)
  waiting for transfers between devices: 663 us -> 172 us
  blocking collectives: 0 us -> 101 us
  matrix products: 95.9 us -> 42.6 us
  starting transfers between devices: 18.4 us -> 37.5 us
  other arithmetic: 27.7 us -> 19.1 us
    all_gather x6 -> x4, waiting for transfers between devices: 470 us -> 52.9 us  [the longest x2 45.6 us: per_device(): full_u = lax.all_gather(u, 'tensor', axis=1, tiled=True)]
    reduce_scatter x5 -> x0, waiting for transfers between devices: 139 us -> none  [per_device(): lax.psum_scatter(partial_value.astype(jnp.bfloat16), 'tensor', scatter_di...]
    all_to_all x0 -> x4, blocking collectives: none -> 81.7 us  [the longest x2 35.7 us: per_device(): u = lax.all_to_all(u, 'dp', 0, 0, tiled=True)]
    all_to_all x1 -> x7, waiting for transfers between devices: 47.6 us -> 115 us  [the longest x2 54.5 us: per_device(): lax.all_to_all(proj.reshape(groups, half, -1), 'dp', 0, 0, tiled=True)]
    dot_general x34, matrix products: 95.9 us -> 42.6 us  [the longest x2 13.6 us: per_device(): proj = jnp.dot(full_u, w_in[layer], preferred_element_type=f32).astype(bf16)]
    all_to_all x1 -> x7, starting transfers between devices: 4.03 us -> 31 us  [the longest x2 9.97 us: per_device(): lax.all_to_all(proj.reshape(groups, half, -1), 'dp', 0, 0, tiled=True)]
    all_gather x0 -> x10, blocking collectives: none -> 19.7 us  [the longest x6 11.2 us: whole(): return lax.all_gather(param, 'section', axis=0, tiled=True)]
    select_n x11 -> x1, other arithmetic: 9.01 us -> 0.01 us  [per_device(): balanced = jnp.zeros((row_count, part), bf16).at[where_to.reshape(-1)].se...]
  transfers between devices with their start and end apart: 17 -> 12, of which waited for: 17 -> 10; matrix products, arithmetic and copies ran while one was open for 2% -> 13% of each run, Pallas kernels for 0% -> 0%
where the time goes in v1:
time: 415 us; the launch traced here: 414 us
  waiting for transfers between devices  172 us (41%)
  blocking collectives  101 us (24%)
  matrix products  42.6 us (10%)
  starting transfers between devices  37.5 us (9%)
  local copies, waits for them, and re-layouts  25.3 us (6%)
  other arithmetic  19.1 us (5%)
  between operations  15.9 us (4%)
    all_to_all x2, waiting for transfers between devices, per_device(): lax.all_to_all(proj.reshape(groups, half, -1), 'dp', 0, 0, tiled=True)  54.5 us
    all_gather x2, waiting for transfers between devices, per_device(): full_u = lax.all_gather(u, 'tensor', axis=1, tiled=True)  45.6 us
    all_to_all x2, blocking collectives, per_device(): u = lax.all_to_all(u, 'dp', 0, 0, tiled=True)  35.7 us
    all_to_all x1, blocking collectives, per_device(): lax.all_to_all(partial_value.reshape(width, few, feats), 'tensor', 0, 0,...  28.4 us
    all_to_all x1, waiting for transfers between devices, per_device(): lax.all_to_all(partial_value.reshape(width, few, feats), 'tensor', 0, 0,...  25.4 us
    all_to_all x1, waiting for transfers between devices, per_device(): lax.all_to_all(outbox.reshape(groups, capacity, part), 'dp', split_axis=0...  24.7 us
    all_to_all x1, blocking collectives, per_device(): outs = lax.all_to_all(outs, ('section', 'tensor'), 0, 0, tiled=True)  17.5 us
    dot_general x2, matrix products, per_device(): proj = jnp.dot(full_u, w_in[layer], preferred_element_type=f32).astype(bf16)  13.6 us
  transfers between devices with their start and end apart: 12, of which 10 were waited for; matrix products, arithmetic and copies ran while one was open for 13% of the time, Pallas kernels for 0%

profile of v1, /device:TPU:0, one launch (start us, length us, event | category | flops | bytes accessed | tf_op | source)
XLA Modules:
  0.0 413.6 jit_solution(3138068230953162979)
XLA Ops:
  9.0 2.0 scatter_custom_fusion
  10.9 6.3 %all-to-all-start = ((s32[4,1,128]{2,1,0:T(1,128)}), s32[4,1,128]{2,1,0:T(1,128)S(1)}, u32[]{:S(2)}, u32[]{:S(2)}) async-start(s32[4,1,128]{2,1,0:T(1,128)} %bitcast.3), calls=%async_computation | async-start | bytes 4096 | tf_op jit(solution)/shard_map/all_to_all | solution.py:80
  17.3 2.6 scatter_custom_fusion.1
  19.9 2.8 all-to-all-done
  22.7 3.5 all-to-all-start.1
  26.3 24.7 %all-to-all-done.1 = bf16[4,128,1024]{2,1,0:T(8,128)(2,1)S(1)} async-done(((bf16[4,128,1024]{2,1,0:T(8,128)(2,1)}), bf16[4,128,1024]{2,1,0:T(8,128)(2,1)S(1)}, u32[]{:S(2)}, u32[]{:S(2)}) %all-to-all-start.1) | async-done | bytes 1048608 | tf_op jit(solution)/shard_map/all_to_all | solution.py:77
  50.9 3.4 scatter_custom_fusion.2
  54.4 3.7 all-to-all-start.2
  58.2 2.0 all-gather
  60.8 6.4 %all-to-all-done.2 = bf16[8,32,1024]{2,1,0:T(8,128)(2,1)S(1)} async-done(((bf16[8,32,1024]{2,1,0:T(8,128)(2,1)}), bf16[8,32,1024]{2,1,0:T(8,128)(2,1)S(1)}, u32[]{:S(2)}, u32[]{:S(2)}) %all-to-all-start.2) | async-done | bytes 524320 | tf_op jit(solution)/shard_map/all_to_all | solution.py:90
  67.9 18.4 %all_to_all.64 = bf16[4,32,2048]{2,1,0:T(8,128)(2,1)} all-to-all(bf16[4,32,2048]{2,1,0:T(8,128)(2,1)S(1)} %fusion.28), channel_id=1, replica_groups=mesh['dp'=4,'section'=2,'tensor'=4] {'dp'}, dimensions={0} | all-to-all | bytes 1048576 | tf_op jit(solution)/shard_map/all_to_all | solution.py:102
  87.9 1.8 all-gather.2
  89.7 1.8 all-gather.1
  91.5 1.8 all-gather.3
  96.2 1.8 all-gather.4
  98.0 2.0 all_gather.47
  102.4 1.3 compare_convert_fusion.4
  107.1 12.1 %all-gather.10.cloned.1.call-done = bf16[4,128,2048]{2,1,0:T(8,128)(2,1)} async-done(((bf16[4,32,2048]{2,1,0:T(8,128)(2,1)}), bf16[4,128,2048]{2,1,0:T(8,128)(2,1)}) %all-gather.10.cloned.1.call-update) | async-done | bytes 2097168 | tf_op jit(solution)/shard_map/all_gather | solution.py:104
  119.2 2.9 fusion.166
  122.0 4.6 %all-to-all-start.5 = ((f32[4,128,8]{1,2,0:T(8,128)}), f32[4,128,8]{1,2,0:T(8,128)S(1)}, u32[]{:S(2)}, u32[]{:S(2)}) async-start(f32[4,128,8]{1,2,0:T(8,128)} %fusion.166), calls=%async_computation.5 | async-start | bytes 32768 | tf_op jit(solution)/shard_map/all_to_all | solution.py:109
  128.5 3.8 all-to-all-done.5
  132.2 1.8 all_gather.48
  136.1 7.3 %all-gather.12.cloned.1.call-done = bf16[2,2048,1280]{2,1,0:T(8,128)(2,1)} async-done(((bf16[1,2048,1280]{2,1,0:T(8,128)(2,1)}), bf16[2,2048,1280]{2,1,0:T(8,128)(2,1)}) %all-gather.12.cloned.1.call-update) | async-done | bytes 10485776 | tf_op jit(solution)/shard_map/all_gather | solution.py:59
  143.4 7.1 %fusion.2 = bf16[512,1280]{1,0:T(8,128)(2,1)} fusion(bf16[512,2048]{1,0:T(8,128)(2,1)} %bitcast.275, bf16[2,2048,1280]{2,1,0:T(8,128)(2,1)} %all-gather.12.cloned.1.call-done), kind=kOutput, calls=%fused_computation.13 | convolution fusion | flops 2685009920 | bytes 8650752 | tf_op jit(solution)/shard_map/dot_general | solution.py:106
  150.5 4.9 %all-to-all-start.4 = ((bf16[4,128,1280]{2,1,0:T(8,128)(2,1)}), bf16[4,128,1280]{2,1,0:T(8,128)(2,1)}, u32[]{:S(2)}, u32[]{:S(2)}) async-start(bf16[4,128,1280]{2,1,0:T(8,128)(2,1)} %bitcast.280), calls=%async_computation.4 | async-start | bytes 2621440 | tf_op jit(solution)/shard_map/all_to_all | solution.py:108
  159.4 27.9 %all-to-all-done.4 = bf16[4,128,1280]{2,1,0:T(8,128)(2,1)} async-done(((bf16[4,128,1280]{2,1,0:T(8,128)(2,1)}), bf16[4,128,1280]{2,1,0:T(8,128)(2,1)}, u32[]{:S(2)}, u32[]{:S(2)}) %all-to-all-start.4) | async-done | bytes 1310752 | tf_op jit(solution)/shard_map/all_to_all | solution.py:108
  187.3 1.5 reduce_sum.113
  188.8 2.5 all_gather.45
  199.2 1.9 convolution_bitcast_fusion.4
  201.1 1.3 fusion.15
  205.0 6.0 %convolution_convert_fusion.1 = bf16[128,8192]{1,0:T(8,128)(2,1)} fusion(bf16[2,512,8192]{2,1,0:T(8,128)(2,1)} %all-gather.14.cloned.1.call-done, f32[128,512]{1,0:T(8,128)S(1)} %get-tuple-element.14, f32[512]{0:T(512)S(1)} %bitcast.326, f32[128]{0:T(128)S(1)} %add_rsqrt_fusion.2), kind=kOutput, calls=%fused_computation.4 | convolution fusion | flops 1074987008 | bytes 10750464 | tf_op jit(solution)/shard_map/dot_general | solution.py:137
  211.0 4.6 %all-to-all-start.6 = ((bf16[4,32,8192]{2,1,0:T(8,128)(2,1)}), bf16[4,32,8192]{2,1,0:T(8,128)(2,1)}, u32[]{:S(2)}, u32[]{:S(2)}) async-start(bf16[4,32,8192]{2,1,0:T(8,128)(2,1)} %bitcast.277), calls=%async_computation.6 | async-start | bytes 4194304 | tf_op jit(solution)/shard_map/all_to_all | solution.py:138
  215.8 25.4 %all-to-all-done.6 = bf16[4,32,8192]{2,1,0:T(8,128)(2,1)} async-done(((bf16[4,32,8192]{2,1,0:T(8,128)(2,1)}), bf16[4,32,8192]{2,1,0:T(8,128)(2,1)}, u32[]{:S(2)}, u32[]{:S(2)}) %all-to-all-start.6) | async-done | bytes 2097184 | tf_op jit(solution)/shard_map/all_to_all | solution.py:138
  241.2 2.0 convert_reduce_fusion.1
  243.2 1.9 reduce_sum.118
  245.0 1.9 multiply_reduce_fusion
  247.2 17.3 %all_to_all.65 = bf16[4,32,2048]{2,1,0:T(8,128)(2,1)} all-to-all(bf16[4,32,2048]{2,1,0:T(8,128)(2,1)S(1)} %get-tuple-element.11), channel_id=1, replica_groups=mesh['dp'=4,'section'=2,'tensor'=4] {'dp'}, dimensions={0} | all-to-all | bytes 1048576 | tf_op jit(solution)/shard_map/all_to_all | solution.py:102
  264.6 33.5 %all-gather.16.cloned.1.call-done = bf16[4,128,2048]{2,1,0:T(8,128)(2,1)} async-done(((bf16[4,32,2048]{2,1,0:T(8,128)(2,1)}), bf16[4,128,2048]{2,1,0:T(8,128)(2,1)}) %all-gather.16.cloned.1.call-update) | async-done | bytes 2097168 | tf_op jit(solution)/shard_map/all_gather | solution.py:104
  298.0 3.0 fusion.164
  301.0 4.6 %all-to-all-start.9 = ((f32[4,128,8]{1,2,0:T(8,128)}), f32[4,128,8]{1,2,0:T(8,128)S(1)}, u32[]{:S(2)}, u32[]{:S(2)}) async-start(f32[4,128,8]{1,2,0:T(8,128)} %fusion.164), calls=%async_computation.9 | async-start | bytes 32768 | tf_op jit(solution)/shard_map/all_to_all | solution.py:109
  305.6 6.4 %fusion.3 = bf16[512,1280]{1,0:T(8,128)(2,1)} fusion(bf16[512,2048]{1,0:T(8,128)(2,1)S(1)} %bitcast.276, bf16[2,2048,1280]{2,1,0:T(8,128)(2,1)} %all-gather.12.cloned.1.call-done), kind=kOutput, calls=%fused_computation.14 | convolution fusion | flops 2685009920 | bytes 8650752 | tf_op jit(solution)/shard_map/dot_general | solution.py:106
  312.1 5.1 %all-to-all-start.8 = ((bf16[4,128,1280]{2,1,0:T(8,128)(2,1)}), bf16[4,128,1280]{2,1,0:T(8,128)(2,1)S(1)}, u32[]{:S(2)}, u32[]{:S(2)}) async-start(bf16[4,128,1280]{2,1,0:T(8,128)(2,1)} %bitcast.279), calls=%async_computation.8 | async-start | bytes 2621440 | tf_op jit(solution)/shard_map/all_to_all | solution.py:108
  317.3 1.8 all_gather.55
  321.3 26.6 %all-to-all-done.8 = bf16[4,128,1280]{2,1,0:T(8,128)(2,1)S(1)} async-done(((bf16[4,128,1280]{2,1,0:T(8,128)(2,1)}), bf16[4,128,1280]{2,1,0:T(8,128)(2,1)S(1)}, u32[]{:S(2)}, u32[]{:S(2)}) %all-to-all-start.8) | async-done | bytes 1310752 | tf_op jit(solution)/shard_map/all_to_all | solution.py:108
  348.1 2.5 all_gather.54
  354.8 4.7 %convolution_convert_fusion = bf16[128,8192]{1,0:T(8,128)(2,1)S(1)} fusion(bf16[2,512,8192]{2,1,0:T(8,128)(2,1)} %all-gather.14.cloned.1.call-done, f32[128,512]{1,0:T(8,128)S(1)} %get-tuple-element.8, f32[512]{0:T(512)S(1)} %bitcast.325, f32[128]{0:T(128)S(1)} %add_rsqrt_fusion), kind=kOutput, calls=%fused_computation.3 | convolution fusion | flops 1074987008 | bytes 10750464 | tf_op jit(solution)/shard_map/dot_general | solution.py:137
  359.5 28.4 %all_to_all.66 = bf16[4,32,8192]{2,1,0:T(8,128)(2,1)S(1)} all-to-all(bf16[4,32,8192]{2,1,0:T(8,128)(2,1)S(1)} %bitcast.278), channel_id=1, replica_groups=mesh['dp'=4,'section'=2,'tensor'=4] {'tensor'}, dimensions={0} | all-to-all | bytes 4194304 | tf_op jit(solution)/shard_map/all_to_all | solution.py:138
  388.5 17.5 %all_to_all.67 = bf16[8,32,2048]{2,1,0:T(8,128)(2,1)S(1)} all-to-all(bf16[8,32,2048]{2,1,0:T(8,128)(2,1)S(1)} %pad_maximum_fusion), channel_id=1, replica_groups=mesh['dp'=4,'section'=2,'tensor'=4] {'section','tensor'}, dimensions={0} | all-to-all | bytes 2097152 | tf_op jit(solution)/shard_map/all_to_all | solution.py:145
  (259 shorter events, 38.5 us)
Async XLA Ops:
  6.5 10.8 %copy-start = (bf16[256,2048]{1,0:T(8,128)(2,1)S(1)}, bf16[256,2048]{1,0:T(8,128)(2,1)}, u32[]{:S(2)}) copy-start(bf16[256,2048]{1,0:T(8,128)(2,1)} %param.11) | copy-start | bytes 3145732
  10.9 11.8 %all-to-all-start = ((s32[4,1,128]{2,1,0:T(1,128)}), s32[4,1,128]{2,1,0:T(1,128)S(1)}, u32[]{:S(2)}, u32[]{:S(2)}) async-start(s32[4,1,128]{2,1,0:T(1,128)} %bitcast.3), calls=%async_computation | async-start | bytes 4096 | tf_op jit(solution)/shard_map/all_to_all | solution.py:80
  19.9 38.2 %copy-start.8 = (f32[1,8192]{1,0:T(1,128)S(1)}, f32[1,8192]{1,0:T(1,128)}, u32[]{:S(2)}) copy-start(f32[1,8192]{1,0:T(1,128)} %param.14) | copy-start | bytes 98308
  22.7 28.2 %all-to-all-start.1 = ((bf16[4,128,1024]{2,1,0:T(8,128)(2,1)}), bf16[4,128,1024]{2,1,0:T(8,128)(2,1)S(1)}, u32[]{:S(2)}, u32[]{:S(2)}) async-start(bf16[4,128,1024]{2,1,0:T(8,128)(2,1)} %bitcast.6), calls=%async_computation.1 | async-start | bytes 2097152 | tf_op jit(solution)/shard_map/all_to_all | solution.py:77
  54.4 12.9 %all-to-all-start.2 = ((bf16[8,32,1024]{2,1,0:T(8,128)(2,1)}), bf16[8,32,1024]{2,1,0:T(8,128)(2,1)S(1)}, u32[]{:S(2)}, u32[]{:S(2)}) async-start(bf16[8,32,1024]{2,1,0:T(8,128)(2,1)} %bitcast.8), calls=%async_computation.2 | async-start | bytes 1048576 | tf_op jit(solution)/shard_map/all_to_all | solution.py:90
  58.1 61.1 %all-gather.10.cloned.1.call-start = ((), (), s32[]{:S(2)}) async-start(), calls=%async_computation.12 | async-start | bytes 2621440 | tf_op jit(solution)/shard_map/all_gather | solution.py:104
  86.3 57.1 %all-gather.12.cloned.1.call-start = ((), (), s32[]{:S(2)}) async-start(), calls=%async_computation.13 | async-start | bytes 15728640 | tf_op jit(solution)/shard_map/all_gather | solution.py:59
  87.1 2.6 copy-start.38
  87.1 4.4 %copy-start.39 = (f32[1,8]{1,0:T(1,128)S(1)}, f32[1,8]{1,0:T(1,128)}, u32[]{:S(2)}) copy-start(f32[1,8]{1,0:T(1,128)} %param.19) | copy-start | bytes 100
  87.1 6.2 %copy-start.29 = (s32[256]{0:T(256)S(1)}, s32[256]{0:T(256)}, u32[]{:S(2)}) copy-start(s32[256]{0:T(256)} %param.13) | copy-start | bytes 3076
  87.1 9.1 %copy-start.32 = (f32[1,512]{1,0:T(1,128)S(1)}, f32[1,512]{1,0:T(1,128)}, u32[]{:S(2)}) copy-start(f32[1,512]{1,0:T(1,128)} %param.20) | copy-start | bytes 6148
  87.1 10.9 %copy-start.6 = (bf16[1,8192,8]{1,2,0:T(8,128)(2,1)S(1)}, bf16[1,8192,8]{1,2,0:T(8,128)(2,1)}, u32[]{:S(2)}) copy-start(bf16[1,8192,8]{1,2,0:T(8,128)(2,1)} %param.16) | copy-start | bytes 393220
  87.1 117.8 %all-gather.14.cloned.1.call-start = ((), (), s32[]{:S(2)}) async-start(), calls=%async_computation.14 | async-start | bytes 25165824 | tf_op jit(solution)/shard_map/all_gather | solution.py:59
  102.4 54.5 %copy-start.19 = (f32[64]{0:T(128)}, f32[64]{0:T(128)S(1)}, u32[]{:S(2)}) copy-start(f32[64]{0:T(128)S(1)} %get-tuple-element.63) | copy-start | bytes 772
  102.4 56.3 %copy-start.17 = (f32[64]{0:T(128)}, f32[64]{0:T(128)S(1)}, u32[]{:S(2)}) copy-start(f32[64]{0:T(128)S(1)} %get-tuple-element.64) | copy-start | bytes 772
  103.7 46.9 %copy-start.27 = (f32[64]{0:T(128)}, f32[64]{0:T(128)S(1)}, u32[]{:S(2)}) copy-start(f32[64]{0:T(128)S(1)} %get-tuple-element.67) | copy-start | bytes 772
  103.7 52.8 %copy-start.25 = (f32[64]{0:T(128)}, f32[64]{0:T(128)S(1)}, u32[]{:S(2)}) copy-start(f32[64]{0:T(128)S(1)} %get-tuple-element.70) | copy-start | bytes 772
  103.7 55.0 %copy-start.21 = (f32[64]{0:T(128)}, f32[64]{0:T(128)S(1)}, u32[]{:S(2)}) copy-start(f32[64]{0:T(128)S(1)} %get-tuple-element.68) | copy-start | bytes 772
  103.7 55.0 %copy-start.23 = (f32[64]{0:T(128)}, f32[64]{0:T(128)S(1)}, u32[]{:S(2)}) copy-start(f32[64]{0:T(128)S(1)} %get-tuple-element.69) | copy-start | bytes 772
  105.7 86.9 %copy-start.15 = (pred[64,64]{1,0:T(8,128)(4,1)}, pred[64,64]{1,0:T(8,128)(4,1)S(1)}, u32[]{:S(2)}) copy-start(pred[64,64]{1,0:T(8,128)(4,1)S(1)} %fusion.173) | copy-start | bytes 12292
  122.0 10.2 %all-to-all-start.5 = ((f32[4,128,8]{1,2,0:T(8,128)}), f32[4,128,8]{1,2,0:T(8,128)S(1)}, u32[]{:S(2)}, u32[]{:S(2)}) async-start(f32[4,128,8]{1,2,0:T(8,128)} %fusion.166), calls=%async_computation.5 | async-start | bytes 32768 | tf_op jit(solution)/shard_map/all_to_all | solution.py:109
  126.6 28.8 %copy-start.30 = (f32[64]{0:T(128)}, f32[64]{0:T(128)S(1)}, u32[]{:S(2)}) copy-start(f32[64]{0:T(128)S(1)} %compare_convert_fusion.2) | copy-start | bytes 772
  150.5 36.8 %all-to-all-start.4 = ((bf16[4,128,1280]{2,1,0:T(8,128)(2,1)}), bf16[4,128,1280]{2,1,0:T(8,128)(2,1)}, u32[]{:S(2)}, u32[]{:S(2)}) async-start(bf16[4,128,1280]{2,1,0:T(8,128)(2,1)} %bitcast.280), calls=%async_computation.4 | async-start | bytes 2621440 | tf_op jit(solution)/shard_map/all_to_all | solution.py:108
  193.8 7.3 %copy-start.9 = (f32[64,8]{0,1:T(8,128)S(1)}, f32[64,8]{0,1:T(8,128)}, u32[]{:S(2)}) copy-start(f32[64,8]{0,1:T(8,128)} %get-tuple-element.40) | copy-start | bytes 6148
  198.3 6.1 %copy-start.11 = (f32[8]{0:T(128)S(1)}, f32[8]{0:T(128)}, u32[]{:S(2)}) copy-start(f32[8]{0:T(128)} %get-tuple-element.52) | copy-start | bytes 100
  202.4 2.3 copy-start.3
  202.4 2.6 copy-start.36
  203.2 1.5 copy-start.4
  203.2 1.5 copy-start.5
  211.0 4.7 %copy-start.7 = (f32[8192]{0:T(1024)S(1)}, f32[8192]{0:T(1024)}, u32[]{:S(2)}) copy-start(f32[8192]{0:T(1024)} %get-tuple-element.5) | copy-start | bytes 98308
  211.0 30.1 %all-to-all-start.6 = ((bf16[4,32,8192]{2,1,0:T(8,128)(2,1)}), bf16[4,32,8192]{2,1,0:T(8,128)(2,1)}, u32[]{:S(2)}, u32[]{:S(2)}) async-start(bf16[4,32,8192]{2,1,0:T(8,128)(2,1)} %bitcast.277), calls=%async_computation.6 | async-start | bytes 4194304 | tf_op jit(solution)/shard_map/all_to_all | solution.py:138
  215.7 82.4 %all-gather.16.cloned.1.call-start = ((), (), s32[]{:S(2)}) async-start(), calls=%async_computation.15 | async-start | bytes 2621440 | tf_op jit(solution)/shard_map/all_gather | solution.py:104
  298.0 7.6 %copy-start.2 = (bf16[4,128,2048]{2,1,0:T(8,128)(2,1)S(1)}, bf16[4,128,2048]{2,1,0:T(8,128)(2,1)}, u32[]{:S(2)}) copy-start(bf16[4,128,2048]{2,1,0:T(8,128)(2,1)} %all-gather.16.cloned.1.call-done) | copy-start | bytes 6291460
  301.0 11.1 %all-to-all-start.9 = ((f32[4,128,8]{1,2,0:T(8,128)}), f32[4,128,8]{1,2,0:T(8,128)S(1)}, u32[]{:S(2)}, u32[]{:S(2)}) async-start(f32[4,128,8]{1,2,0:T(8,128)} %fusion.164), calls=%async_computation.9 | async-start | bytes 32768 | tf_op jit(solution)/shard_map/all_to_all | solution.py:109
  312.1 7.0 %copy-start.33 = (f32[8]{0:T(128)S(1)}, f32[8]{0:T(128)}, u32[]{:S(2)}) copy-start(f32[8]{0:T(128)} %get-tuple-element.53) | copy-start | bytes 100
  312.1 7.0 %copy-start.34 = (f32[8]{0:T(128)S(1)}, f32[8]{0:T(128)}, u32[]{:S(2)}) copy-start(f32[8]{0:T(128)} %get-tuple-element.55) | copy-start | bytes 100
  312.1 7.4 %copy-start.28 = (f32[64]{0:T(128)S(1)}, f32[64]{0:T(128)}, u32[]{:S(2)}) copy-start(f32[64]{0:T(128)} %copy-done.27) | copy-start | bytes 772
  312.1 7.8 %copy-start.31 = (f32[64]{0:T(128)S(1)}, f32[64]{0:T(128)}, u32[]{:S(2)}) copy-start(f32[64]{0:T(128)} %copy-done.30) | copy-start | bytes 772
  312.1 8.3 %copy-start.26 = (f32[64]{0:T(128)S(1)}, f32[64]{0:T(128)}, u32[]{:S(2)}) copy-start(f32[64]{0:T(128)} %copy-done.25) | copy-start | bytes 772
  312.1 8.8 %copy-start.20 = (f32[64]{0:T(128)S(1)}, f32[64]{0:T(128)}, u32[]{:S(2)}) copy-start(f32[64]{0:T(128)} %copy-done.19) | copy-start | bytes 772
  312.1 9.0 %copy-start.18 = (f32[64]{0:T(128)S(1)}, f32[64]{0:T(128)}, u32[]{:S(2)}) copy-start(f32[64]{0:T(128)} %copy-done.17) | copy-start | bytes 772
  312.1 9.0 %copy-start.22 = (f32[64]{0:T(128)S(1)}, f32[64]{0:T(128)}, u32[]{:S(2)}) copy-start(f32[64]{0:T(128)} %copy-done.21) | copy-start | bytes 772
  312.1 9.0 %copy-start.24 = (f32[64]{0:T(128)S(1)}, f32[64]{0:T(128)}, u32[]{:S(2)}) copy-start(f32[64]{0:T(128)} %copy-done.23) | copy-start | bytes 772
  312.1 35.7 %all-to-all-start.8 = ((bf16[4,128,1280]{2,1,0:T(8,128)(2,1)}), bf16[4,128,1280]{2,1,0:T(8,128)(2,1)S(1)}, u32[]{:S(2)}, u32[]{:S(2)}) async-start(bf16[4,128,1280]{2,1,0:T(8,128)(2,1)} %bitcast.279), calls=%async_computation.8 | async-start | bytes 2621440 | tf_op jit(solution)/shard_map/all_to_all | solution.py:108
  321.2 30.4 %copy-start.16 = (pred[64,64]{1,0:T(8,128)(4,1)S(1)}, pred[64,64]{1,0:T(8,128)(4,1)}, u32[]{:S(2)}) copy-start(pred[64,64]{1,0:T(8,128)(4,1)} %copy-done.15) | copy-start | bytes 12292
  348.1 3.9 copy-start.10
  350.7 1.8 copy-start.14
  388.4 18.6 %copy-start.1 = (bf16[256,2048]{1,0:T(8,128)(2,1)S(1)}, bf16[256,2048]{1,0:T(8,128)(2,1)}, u32[]{:S(2)}) copy-start(bf16[256,2048]{1,0:T(8,128)(2,1)} %param.11) | copy-start | bytes 3145732
  (4 other events, 4.6 us)
Sparse Core Ops, SparseCore 0:
  86.4 32.6 all-gather.9
  120.7 22.6 all-gather.11
  144.9 31.2 all-gather.13
  264.7 33.2 all-gather.15

commit v2 on v1

v2 whole, which is shorter than its diff:
```python
import jax
import jax.numpy as jnp
from jax import lax
from jax.sharding import PartitionSpec as P

HEAD_DIM = 64
STATE = 128
HEADS_DEV = 8


epsilon = 1e-05


def scan_block(inputs, writes, readout, step_size, log_decay, resets, state, skips):
    segment = jnp.cumsum(resets)
    cumulative = jnp.cumsum(log_decay, axis=0)
    positions = jnp.arange(resets.shape[0])
    in_segment = (segment[:, None] == segment[None, :]) & (positions[:, None] >= positions[None, :])
    by_head = cumulative.T
    gap = by_head[:, :, None] - by_head[:, None, :]
    decayed = jnp.where(in_segment[None], jnp.exp(jnp.where(in_segment[None], gap, 0.0)), 0.0)
    f32 = jnp.float32
    scores = jnp.einsum("tn,sn->ts", readout, writes, preferred_element_type=f32)
    weights = scores[None] * decayed * step_size.T[:, None, :]
    output = jnp.einsum("hts,shp->thp", weights, inputs.astype(f32))
    carry_ok = (segment == 0).astype(f32)
    carried = jnp.einsum("tn,hpn->thp", readout.astype(f32), state)
    output = output + carry_ok[:, None, None] * jnp.exp(cumulative)[:, :, None] * carried
    last_seg = segment[-1]
    tail = (
        (segment == last_seg).astype(f32)[:, None]
        * jnp.exp(cumulative[-1][None, :] - cumulative)
        * step_size
    )
    fresh = jnp.einsum("shp,sn->hpn", tail[:, :, None] * inputs.astype(f32), writes.astype(f32))
    kept = (last_seg == 0).astype(f32) * jnp.exp(cumulative[-1])[:, None, None] * state
    output = output + skips[None, :, None] * inputs.astype(f32)
    return (output, fresh + kept)


CHUNKS = 2


def shift(block, axis, distance):
    n = lax.axis_size(axis)
    return lax.ppermute(block, axis, [(i, (i + distance) % n) for i in range(n)])


def exchange(blocks, axis):
    return [b if k == 0 else shift(b, axis, k) for k, b in enumerate(blocks)]


def turned(stack, start):
    n = stack.shape[0]
    return lax.dynamic_slice_in_dim(jnp.concatenate([stack, stack], axis=0), start, n, axis=0)


def in_order(stack, me):
    n = stack.shape[0]
    return turned(stack[::-1], n - 1 - me)


def per_device(
    tokens, dest_slot, doc_reset, norm_gain, w_in, w_step, step_bias, a_log, d_skip, out_gain, w_out
):
    f32, bf16 = jnp.float32, jnp.bfloat16
    groups = lax.axis_size("dp")
    width = lax.axis_size("tensor")
    cores = lax.axis_size("section")
    group, lane, core = lax.axis_index("dp"), lax.axis_index("tensor"), lax.axis_index("section")
    row_count, feat_local = tokens.shape
    feats = feat_local * width
    depth = w_in.shape[1]
    head_cols = HEADS_DEV * HEAD_DIM
    half = row_count // cores
    src_few = half // width
    few = half // (CHUNKS * width)
    part = few * width

    w_in = lax.all_gather(w_in, "section", axis=0, tiled=True)
    step_own = lax.dynamic_slice_in_dim(w_step[0], group * depth, depth, axis=0)
    w_step = lax.all_gather(step_own, "section", axis=0)
    small = [norm_gain[0], step_bias[0], a_log[0], d_skip[0], out_gain[0]]
    joined = lax.all_gather(jnp.concatenate(small), "section", axis=0)
    params, at = [], 0
    for piece in small:
        params.append(joined[:, at : at + piece.shape[0]])
        at += piece.shape[0]
    norm_gain, step_bias, a_log, d_skip, out_gain = params
    w_out = lax.all_gather(w_out, "section", axis=0, tiled=True)

    mine = lax.dynamic_slice_in_dim(tokens, core * half, half, axis=0)
    mine = lax.all_to_all(mine.reshape(width, src_few, feat_local), "tensor", 0, 0, tiled=True)
    mine = mine.transpose(1, 0, 2).reshape(src_few, groups, depth).transpose(1, 0, 2)
    mine = lax.all_to_all(mine, "dp", 0, 0, tiled=True)
    parts = exchange([mine] * width, "tensor")
    others = [shift(p, "section", 1) for p in parts]
    pool = jnp.stack(parts + others).reshape(-1, depth)

    slots = lax.all_gather(dest_slot, "dp", axis=0, tiled=True)
    source_of = jnp.zeros_like(slots).at[slots].set(jnp.arange(slots.shape[0], dtype=jnp.int32))
    source_of = source_of.reshape(groups, CHUNKS, cores, part)
    source_of = lax.dynamic_index_in_dim(source_of, core, 2, keepdims=False)
    source_of = turned(source_of, group).transpose(1, 0, 2)
    src_group, inner = source_of // row_count, source_of % row_count
    src_core, inner = inner // half, inner % half
    src_lane, inner = inner // src_few, inner % src_few
    place = (core - src_core) % cores * width + (lane - src_lane) % width
    place = (place * groups + src_group) * src_few + inner
    first = pool[place.reshape(-1)].reshape(CHUNKS, groups, part, depth)
    gain_own = lax.dynamic_slice_in_dim(norm_gain[0], group * depth, depth)

    def project(rows, layer):
        flat = rows.reshape(groups * part, depth)
        proj = jnp.dot(flat, w_in[layer], preferred_element_type=f32).astype(bf16)
        pre = jnp.dot(flat, w_step[layer], preferred_element_type=f32)
        return proj.reshape(groups, part, -1), pre.reshape(groups, part, -1)

    def added(blocks):
        return sum(b.astype(f32) for b in blocks)

    def mix(proj, pre, resets, state, layer):
        proj = lax.all_gather(proj, "section", axis=0, tiled=True)
        pre = lax.all_gather(pre, "section", axis=0, tiled=True)
        count = proj.shape[0]
        step_size = jax.nn.softplus(pre + step_bias[layer])
        log_decay = -jnp.exp(a_log[layer]) * step_size
        mixed, state = scan_block(
            proj[:, head_cols : 2 * head_cols].reshape(count, HEADS_DEV, HEAD_DIM),
            proj[:, 2 * head_cols : 2 * head_cols + STATE],
            proj[:, 2 * head_cols + STATE :],
            step_size,
            log_decay,
            resets,
            state,
            d_skip[layer],
        )
        mixed = mixed.reshape(count, head_cols)
        mixed = lax.dynamic_slice_in_dim(mixed, core * part, part, axis=0)
        gate = lax.dynamic_slice_in_dim(proj[:, :head_cols], core * part, part, axis=0).astype(f32)
        gated = mixed * jax.nn.silu(gate)
        meansq_out = jnp.mean(gated * gated, axis=-1, keepdims=True)
        normed = (gated * lax.rsqrt(meansq_out + epsilon) * out_gain[layer]).astype(bf16)
        normed = turned(normed.reshape(width, few, head_cols), lane).reshape(part, head_cols)
        partial_value = jnp.dot(normed, w_out[layer], preferred_element_type=f32).astype(bf16)
        blocks = partial_value.reshape(width, few, feats)
        return added(exchange([blocks[k] for k in range(width)], "tensor")), state

    def delivered(rows, layer):
        blocks = turned(rows.reshape(few, width, feat_local).transpose(1, 0, 2), lane)
        own = jnp.stack(exchange([blocks[k] for k in range(width)], "tensor"))
        own = in_order(own, lane).reshape(part, feat_local)
        return own, lax.ppermute(own, "section", [(cores - 1 - layer, layer)])

    resets = doc_reset.reshape(CHUNKS, -1)
    zero_state = jnp.zeros((HEADS_DEV, HEAD_DIM, STATE), f32)
    sent = []
    for c in range(CHUNKS):
        wide = first[c].astype(f32)
        squares = jnp.sum(wide * wide, axis=-1)
        proj, pre = project((wide * gain_own).astype(bf16), 0)
        side = jnp.concatenate([pre, squares[:, :, None]], axis=-1)
        kept = lax.dynamic_slice_in_dim(first[c], lane * few, few, axis=1)
        proj = exchange([proj[k] for k in range(groups)], "dp")
        side = exchange([side[k] for k in range(groups)], "dp")
        kept = exchange([kept[k] for k in range(groups)], "dp")
        sent.append((proj, side, kept))
    state = zero_state
    middle, outs = [], []
    for c in range(CHUNKS):
        proj, side, kept = sent[c]
        side = added(side)
        scale = lax.rsqrt(side[:, HEADS_DEV:] / feats + epsilon)
        summed, state = mix(
            (added(proj) * scale).astype(bf16), side[:, :HEADS_DEV] * scale, resets[c], state, 0
        )
        kept = in_order(jnp.stack(kept), group).transpose(1, 0, 2).reshape(few, feats)
        rows = (kept.astype(f32) + summed).astype(bf16)
        middle.append(rows)
        widened = rows.astype(f32)
        meansq = jnp.mean(widened * widened, axis=-1, keepdims=True)
        u = (widened * lax.rsqrt(meansq + epsilon) * norm_gain[1]).astype(bf16)
        u = turned(u.reshape(few, groups, depth).transpose(1, 0, 2), group)
        u = jnp.stack(exchange([u[k] for k in range(groups)], "dp"))
        u = jnp.stack(exchange([u] * width, "tensor"), axis=1)
        proj, pre = project(u, 1)
        back = [(groups - k) % groups for k in range(groups)]
        proj = exchange([proj[k] for k in back], "dp")
        pre = exchange([pre[k] for k in back], "dp")
        sent[c] = (proj, pre)
    state = zero_state
    for c in range(CHUNKS):
        proj, pre = sent[c]
        proj = in_order(added(proj).astype(bf16).reshape(width, few, -1), lane).reshape(part, -1)
        pre = in_order(added(pre).reshape(width, few, -1), lane).reshape(part, -1)
        summed, state = mix(proj, pre, resets[c], state, 1)
        rows = (middle[c].astype(f32) + summed).astype(bf16)
        own_a, got_a = delivered(middle[c], 0)
        own_b, got_b = delivered(rows, 1)
        outs.append(jnp.where(core == 0, own_a, got_b))
        outs.append(jnp.where(core == 0, got_a, own_b))
    return jnp.concatenate(outs, axis=0)[None]


def solution(mesh):
    placed = (
        P("dp", "tensor"),
        P("dp"),
        P("dp"),
        P("section", None),
        P("section", "dp", "tensor"),
        P("section", None, "tensor"),
        P("section", "tensor"),
        P("section", "tensor"),
        P("section", "tensor"),
        P("section", "tensor"),
        P("section", "tensor", None),
    )
    return jax.shard_map(
        per_device,
        mesh=mesh,
        in_specs=placed,
        out_specs=P("section", "dp", "tensor"),
        check_vma=False,
    )
```

time: 415 us -> 371 us (0.89)
  starting transfers between devices: 37.5 us -> 110 us
  blocking collectives: 101 us -> 29.1 us
  waiting for transfers between devices: 172 us -> 109 us
  local copies, waits for them, and re-layouts: 25.3 us -> 38.3 us
  other arithmetic: 19.1 us -> 25.9 us
    all_to_all x8 -> x2, waiting for transfers between devices: 118 us -> 13.8 us  [the longest x1 13.8 us: per_device(): mine = lax.all_to_all(mine, 'dp', 0, 0, tiled=True)]
    ppermute x0 -> x77, starting transfers between devices: none -> 101 us  [the longest x73 95.4 us: shift(): lax.ppermute(block, axis, [(i, (i + distance) % n) for i in range(n)])]
    ppermute x0 -> x77, waiting for transfers between devices: none -> 93.8 us  [the longest x73 93.8 us: shift(): lax.ppermute(block, axis, [(i, (i + distance) % n) for i in range(n)])]
    all_to_all x4 -> x0, blocking collectives: 81.7 us -> none  [the longest x2 35.7 us: per_device(): u = lax.all_to_all(u, 'dp', 0, 0, tiled=True)]
    all_gather x4 -> x2, waiting for transfers between devices: 52.9 us -> 0.04 us  [the longest x1 0.02 us: per_device(): w_out = lax.all_gather(w_out, 'section', axis=0, tiled=True)]
    all_to_all x8 -> x2, starting transfers between devices: 37.4 us -> 8.71 us  [the longest x1 5.19 us: per_device(): lax.all_to_all(mine.reshape(width, src_few, feat_local), 'tensor', 0, 0,...]
    all_gather x10, blocking collectives: 19.7 us -> 29.1 us  [the longest x1 11.6 us: per_device(): slots = lax.all_gather(dest_slot, 'dp', axis=0, tiled=True)]
    unnamed x81 -> x60, local copies, waits for them, and re-layouts: 1.15 us -> 10 us
  transfers between devices with their start and end apart: 12 -> 82, of which waited for: 10 -> 29; matrix products, arithmetic and copies ran while one was open for 13% -> 26% of each run, Pallas kernels for 0% -> 0%
where the time goes in v2:
time: 371 us; the launch traced here: 370 us
  starting transfers between devices  110 us (30%)
  waiting for transfers between devices  109 us (29%)
  matrix products  42.3 us (11%)
  local copies, waits for them, and re-layouts  38.3 us (10%)
  blocking collectives  29.1 us (8%)
  other arithmetic  25.9 us (7%)
  between operations  15.7 us (4%)
    ppermute x73, starting transfers between devices, shift(): lax.ppermute(block, axis, [(i, (i + distance) % n) for i in range(n)])  95.4 us
    ppermute x73, waiting for transfers between devices, shift(): lax.ppermute(block, axis, [(i, (i + distance) % n) for i in range(n)])  93.8 us
    dot_general x4, matrix products, mix(): jnp.dot(normed, w_out[layer], preferred_element_type=f32).astype(bf16)  19.8 us
    all_to_all x1, waiting for transfers between devices, per_device(): mine = lax.all_to_all(mine, 'dp', 0, 0, tiled=True)  13.8 us
    dot_general x4, matrix products, project(): proj = jnp.dot(flat, w_in[layer], preferred_element_type=f32).astype(bf16)  13.7 us
    all_gather x1, blocking collectives, per_device(): slots = lax.all_gather(dest_slot, 'dp', axis=0, tiled=True)  11.6 us
    unnamed x60, local copies, waits for them, and re-layouts  10 us
    all_gather x4, blocking collectives, mix(): proj = lax.all_gather(proj, 'section', axis=0, tiled=True)  8.16 us
  transfers between devices with their start and end apart: 82, of which 29 were waited for; matrix products, arithmetic and copies ran while one was open for 26% of the time, Pallas kernels for 0%

profile of v2, /device:TPU:0, one launch (start us, length us, event | category | flops | bytes accessed | tf_op | source)
XLA Modules:
  0.0 369.9 jit_solution(5074055692245729169)
XLA Ops:
  12.2 5.2 %all-to-all-start = ((bf16[4,32,2048]{2,1,0:T(8,128)(2,1)}), bf16[4,32,2048]{2,1,0:T(8,128)(2,1)}, u32[]{:S(2)}, u32[]{:S(2)}) async-start(bf16[4,32,2048]{2,1,0:T(8,128)(2,1)} %bitcast), calls=%async_computation | async-start | bytes 1048576 | tf_op jit(solution)/shard_map/all_to_all | solution.py:93
  19.1 11.6 %all-gather.1 = s32[4,1,256]{2,1,0:T(1,128)S(1)} all-gather(s32[1,1,256]{2,1,0:T(1,128)S(1)} %bitcast.458), channel_id=1, replica_groups=mesh['dp'=4,'section'=2,'tensor'=4] {'dp'}, dimensions={0}, use_global_device_ids=true | all-gather | bytes 5120 | tf_op jit(solution)/shard_map/all_gather | solution.py:100
  30.8 4.3 %scatter_custom_fusion = s32[1024]{0:T(1024)S(1)} fusion(s32[1024]{0:T(1024)S(1)} %compare_select_fusion.5, s32[1024]{0:T(1024)S(1)} %iota.29, s32[]{:T(128)} %constant.144.clone.1), kind=kCustom, calls=%fused_computation.404 | custom fusion | bytes 4100 | tf_op jit(solution)/shard_map/scatter | solution.py:101
  43.2 3.5 all-to-all-start.1
  48.0 13.8 %all-to-all-done.1 = bf16[4,32,2048]{2,1,0:T(8,128)(2,1)S(1)} async-done(((bf16[4,32,2048]{2,1,0:T(8,128)(2,1)}), bf16[4,32,2048]{2,1,0:T(8,128)(2,1)S(1)}, u32[]{:S(2)}, u32[]{:S(2)}) %all-to-all-start.1) | async-done | bytes 524320 | tf_op jit(solution)/shard_map/all_to_all | solution.py:95
  68.2 9.3 %collective-permute-done = bf16[4,32,2048]{2,1,0:T(8,128)(2,1)S(1)} collective-permute-done((bf16[4,32,2048]{2,1,0:T(8,128)(2,1)S(1)}, bf16[4,32,2048]{2,1,0:T(8,128)(2,1)S(1)}, u32[]{:S(2)}, u32[]{:S(2)}) %collective-permute-start) | collective-permute-done | bytes 524320 | tf_op jit(solution)/shard_map/ppermute | solution.py:46
  78.4 8.9 %collective-permute-done.1 = bf16[4,32,2048]{2,1,0:T(8,128)(2,1)S(1)} collective-permute-done((bf16[4,32,2048]{2,1,0:T(8,128)(2,1)S(1)}, bf16[4,32,2048]{2,1,0:T(8,128)(2,1)S(1)}, u32[]{:S(2)}, u32[]{:S(2)}) %collective-permute-start.1) | collective-permute-done | bytes 524320 | tf_op jit(solution)/shard_map/ppermute | solution.py:46
  92.8 7.1 %gather_fusion = bf16[512,2048]{1,0:T(8,128)(2,1)S(1)} fusion(bf16[1024,2048]{1,0:T(8,128)(2,1)} %bitcast.9, s32[1024]{0:T(1024)S(1)} %pad_clamp_fusion), kind=kCustom, calls=%fused_computation | custom fusion | bytes 4196352 | tf_op jit(solution)/shard_map/gather | solution.py:110
  107.2 2.4 collective-permute-start.48
  109.6 2.4 collective-permute-start.50
  114.4 2.5 collective-permute-start.14
  135.6 2.4 collective-permute-done.44
  139.2 4.1 %fusion.7 = bf16[256,1280]{1,0:T(8,128)(2,1)S(1)} fusion(bf16[256,2048]{1,0:T(8,128)(2,1)S(1)} %copy-done.2, bf16[2,2048,1280]{2,1,0:T(8,128)(2,1)} %all-gather.9.cloned.1.call-done), kind=kOutput, calls=%fused_computation.21 | convolution fusion | flops 1342504960 | bytes 6946816 | tf_op jit(solution)/shard_map/dot_general | solution.py:115
  144.4 2.4 collective-permute-start.46
  152.3 2.2 collective-permute-start.12
  154.5 8.1 %collective-permute-done.46 = bf16[64,1280]{1,0:T(8,128)(2,1)S(1)} collective-permute-done((bf16[64,1280]{1,0:T(8,128)(2,1)S(1)}, bf16[64,1280]{1,0:T(8,128)(2,1)S(1)}, u32[]{:S(2)}, u32[]{:S(2)}) %collective-permute-start.46) | collective-permute-done | bytes 163872 | tf_op jit(solution)/shard_map/ppermute | solution.py:46
  164.9 6.6 %collective-permute-done.11 = bf16[64,1280]{1,0:T(8,128)(2,1)S(1)} collective-permute-done((bf16[64,1280]{1,0:T(8,128)(2,1)S(1)}, bf16[64,1280]{1,0:T(8,128)(2,1)S(1)}, u32[]{:S(2)}, u32[]{:S(2)}) %collective-permute-start.11) | collective-permute-done | bytes 163872 | tf_op jit(solution)/shard_map/ppermute | solution.py:46
  180.5 5.0 %convolution_convert_fusion.3 = bf16[64,8192]{1,0:T(8,128)(2,1)S(1)} fusion(bf16[64,512]{1,0:T(8,128)(2,1)S(1)} %bitcast.433, bf16[2,512,8192]{2,1,0:T(8,128)(2,1)} %all-gather.11.cloned.1.call-done), kind=kOutput, calls=%fused_computation.5 | convolution fusion | flops 537395200 | bytes 9502720 | tf_op jit(solution)/shard_map/dot_general | solution.py:145
  185.5 2.7 collective-permute-start.16
  190.2 4.9 %convolution_convert_fusion.1 = bf16[64,8192]{1,0:T(8,128)(2,1)S(1)} fusion(bf16[64,512]{1,0:T(8,128)(2,1)S(1)} %bitcast.432, bf16[2,512,8192]{2,1,0:T(8,128)(2,1)} %all-gather.11.cloned.1.call-done), kind=kOutput, calls=%fused_computation.3 | convolution fusion | flops 537395200 | bytes 9502720 | tf_op jit(solution)/shard_map/dot_general | solution.py:145
  198.5 2.8 collective-permute-done.17
  201.9 5.1 %collective-permute-done.51 = bf16[16,8192]{1,0:T(8,128)(2,1)S(1)} collective-permute-done((bf16[16,8192]{1,0:T(8,128)(2,1)S(1)}, bf16[16,8192]{1,0:T(8,128)(2,1)S(1)}, u32[]{:S(2)}, u32[]{:S(2)}) %collective-permute-start.51) | collective-permute-done | bytes 262176 | tf_op jit(solution)/shard_map/ppermute | solution.py:46
  207.0 4.7 %collective-permute-done.52 = bf16[16,8192]{1,0:T(8,128)(2,1)S(1)} collective-permute-done((bf16[16,8192]{1,0:T(8,128)(2,1)S(1)}, bf16[16,8192]{1,0:T(8,128)(2,1)S(1)}, u32[]{:S(2)}, u32[]{:S(2)}) %collective-permute-start.52) | collective-permute-done | bytes 262176 | tf_op jit(solution)/shard_map/ppermute | solution.py:46
  212.8 3.8 %collective-permute-start.57 = (bf16[16,2048]{1,0:T(8,128)(2,1)S(1)}, bf16[16,2048]{1,0:T(8,128)(2,1)S(1)}, u32[]{:S(2)}, u32[]{:S(2)}) collective-permute-start(bf16[16,2048]{1,0:T(8,128)(2,1)S(1)} %get-tuple-element.79), channel_id=1, source_target_pairs={{0,8},{8,16},{16,24},{24,0},{1,9},{9,17},{17,25},{25,1},{2,10},{10... | collective-permute-start | bytes 196616 | tf_op jit(solution)/shard_map/ppermute | solution.py:46
  223.1 2.2 collective-permute-start.59
  225.3 2.1 collective-permute-start.23
  235.4 2.1 collective-permute-start.62
  239.8 3.7 collective-permute-done.60
  244.5 6.4 %collective-permute-done.61 = bf16[4,16,2048]{2,1,0:T(8,128)(2,1)} collective-permute-done((bf16[4,16,2048]{2,1,0:T(8,128)(2,1)S(1)}, bf16[4,16,2048]{2,1,0:T(8,128)(2,1)}, u32[]{:S(2)}, u32[]{:S(2)}) %collective-permute-start.61) | collective-permute-done | bytes 262176 | tf_op jit(solution)/shard_map/ppermute | solution.py:46
  255.1 4.0 %fusion.5 = bf16[256,1280]{1,0:T(8,128)(2,1)S(1)} fusion(bf16[256,2048]{1,0:T(8,128)(2,1)S(1)} %bitcast.370, bf16[2,2048,1280]{2,1,0:T(8,128)(2,1)} %all-gather.9.cloned.1.call-done), kind=kOutput, calls=%fused_computation.19 | convolution fusion | flops 1342504960 | bytes 6946816 | tf_op jit(solution)/shard_map/dot_general | solution.py:115
  261.2 3.0 collective-permute-start.68
  265.8 4.0 %fusion.4 = bf16[256,1280]{1,0:T(8,128)(2,1)S(1)} fusion(bf16[256,2048]{1,0:T(8,128)(2,1)S(1)} %bitcast.373, bf16[2,2048,1280]{2,1,0:T(8,128)(2,1)} %all-gather.9.cloned.1.call-done), kind=kOutput, calls=%fused_computation.18 | convolution fusion | flops 1342504960 | bytes 6946816 | tf_op jit(solution)/shard_map/dot_general | solution.py:115
  272.8 2.9 collective-permute-start.33
  279.3 2.9 collective-permute-start.65
  287.2 4.3 %collective-permute-start.28 = (bf16[64,1280]{1,0:T(8,128)(2,1)}, bf16[64,1280]{1,0:T(8,128)(2,1)}, u32[]{:S(2)}, u32[]{:S(2)}) collective-permute-start(bf16[64,1280]{1,0:T(8,128)(2,1)} %get-tuple-element.37), channel_id=1, source_target_pairs={{0,8},{8,16},{16,24},{24,0},{1,9},{9,17},{17,25},{25,1},{2,10},{10... | collective-permute-start | bytes 491528 | tf_op jit(solution)/shard_map/ppermute | solution.py:46
  291.5 2.2 collective-permute-done.64
  293.7 5.2 %collective-permute-start.30 = (bf16[64,1280]{1,0:T(8,128)(2,1)}, bf16[64,1280]{1,0:T(8,128)(2,1)}, u32[]{:S(2)}, u32[]{:S(2)}) collective-permute-start(bf16[64,1280]{1,0:T(8,128)(2,1)} %get-tuple-element.38), channel_id=1, source_target_pairs={{0,24},{8,0},{16,8},{24,16},{1,25},{9,1},{17,9},{25,17},{2,26},{10... | collective-permute-start | bytes 491528 | tf_op jit(solution)/shard_map/ppermute | solution.py:46
  301.3 6.2 %collective-permute-done.29 = bf16[64,1280]{1,0:T(8,128)(2,1)} collective-permute-done((bf16[64,1280]{1,0:T(8,128)(2,1)}, bf16[64,1280]{1,0:T(8,128)(2,1)}, u32[]{:S(2)}, u32[]{:S(2)}) %collective-permute-start.29) | collective-permute-done | bytes 163872 | tf_op jit(solution)/shard_map/ppermute | solution.py:46
  307.5 2.9 collective-permute-done.30
  316.4 5.0 %convolution_convert_fusion.2 = bf16[64,8192]{1,0:T(8,128)(2,1)S(1)} fusion(bf16[64,512]{1,0:T(8,128)(2,1)S(1)} %bitcast.435, bf16[2,512,8192]{2,1,0:T(8,128)(2,1)} %all-gather.11.cloned.1.call-done), kind=kOutput, calls=%fused_computation.4 | convolution fusion | flops 537395200 | bytes 9502720 | tf_op jit(solution)/shard_map/dot_general | solution.py:145
  321.6 2.8 collective-permute-start.36
  324.5 5.0 %convolution_convert_fusion = bf16[64,8192]{1,0:T(8,128)(2,1)S(1)} fusion(bf16[64,512]{1,0:T(8,128)(2,1)S(1)} %bitcast.434, bf16[2,512,8192]{2,1,0:T(8,128)(2,1)} %all-gather.11.cloned.1.call-done), kind=kOutput, calls=%fused_computation.2 | convolution fusion | flops 537395200 | bytes 9502720 | tf_op jit(solution)/shard_map/dot_general | solution.py:145
  331.6 3.9 %collective-permute-done.35 = bf16[16,8192]{1,0:T(8,128)(2,1)S(1)} collective-permute-done((bf16[16,8192]{1,0:T(8,128)(2,1)S(1)}, bf16[16,8192]{1,0:T(8,128)(2,1)S(1)}, u32[]{:S(2)}, u32[]{:S(2)}) %collective-permute-start.35) | collective-permute-done | bytes 262176 | tf_op jit(solution)/shard_map/ppermute | solution.py:46
  335.6 2.8 collective-permute-start.71
  338.8 4.1 %collective-permute-done.69 = bf16[16,8192]{1,0:T(8,128)(2,1)S(1)} collective-permute-done((bf16[16,8192]{1,0:T(8,128)(2,1)S(1)}, bf16[16,8192]{1,0:T(8,128)(2,1)S(1)}, u32[]{:S(2)}, u32[]{:S(2)}) %collective-permute-start.69) | collective-permute-done | bytes 262176 | tf_op jit(solution)/shard_map/ppermute | solution.py:46
  342.9 5.4 %collective-permute-done.70 = bf16[16,8192]{1,0:T(8,128)(2,1)S(1)} collective-permute-done((bf16[16,8192]{1,0:T(8,128)(2,1)S(1)}, bf16[16,8192]{1,0:T(8,128)(2,1)S(1)}, u32[]{:S(2)}, u32[]{:S(2)}) %collective-permute-start.70) | collective-permute-done | bytes 262176 | tf_op jit(solution)/shard_map/ppermute | solution.py:46
  348.4 3.2 collective-permute-start.39
  354.0 2.7 collective-permute-start.74
  (399 shorter events, 139.0 us)
Async XLA Ops:
  6.5 35.6 %all-reduce.3.cloned.1.call-start = ((), (), s32[]{:S(2)}) async-start(), calls=%async_computation.4 | async-start | bytes 147456
  10.6 128.5 %all-gather.9.cloned.1.call-start = ((), (), s32[]{:S(2)}) async-start(), calls=%async_computation.2 | async-start | bytes 15728640 | tf_op jit(solution)/shard_map/all_gather | solution.py:80
  12.2 31.0 %all-to-all-start = ((bf16[4,32,2048]{2,1,0:T(8,128)(2,1)}), bf16[4,32,2048]{2,1,0:T(8,128)(2,1)}, u32[]{:S(2)}, u32[]{:S(2)}) async-start(bf16[4,32,2048]{2,1,0:T(8,128)(2,1)} %bitcast), calls=%async_computation | async-start | bytes 1048576 | tf_op jit(solution)/shard_map/all_to_all | solution.py:93
  17.4 163.0 %all-gather.11.cloned.1.call-start = ((), (), s32[]{:S(2)}) async-start(), calls=%async_computation.3 | async-start | bytes 25165824 | tf_op jit(solution)/shard_map/all_gather | solution.py:90
  43.2 18.6 %all-to-all-start.1 = ((bf16[4,32,2048]{2,1,0:T(8,128)(2,1)}), bf16[4,32,2048]{2,1,0:T(8,128)(2,1)S(1)}, u32[]{:S(2)}, u32[]{:S(2)}) async-start(bf16[4,32,2048]{2,1,0:T(8,128)(2,1)} %all-to-all-done), calls=%async_computation.1 | async-start | bytes 1048576 | tf_op jit(solution)/shard_map/all_to_all | solution.py:95
  61.8 15.7 %collective-permute-start = (bf16[4,32,2048]{2,1,0:T(8,128)(2,1)S(1)}, bf16[4,32,2048]{2,1,0:T(8,128)(2,1)S(1)}, u32[]{:S(2)}, u32[]{:S(2)}) collective-permute-start(bf16[4,32,2048]{2,1,0:T(8,128)(2,1)S(1)} %all-to-all-done.1), channel_id=1, source_target_pairs={{0,1},{1,2},{2,3},{3,0},{4,5},{5,6},{6,7},{7,4},{8,9},{9,10},{10,1... | collective-permute-start | bytes 1572872 | tf_op jit(solution)/shard_map/ppermute | solution.py:46
  64.4 22.9 %collective-permute-start.1 = (bf16[4,32,2048]{2,1,0:T(8,128)(2,1)S(1)}, bf16[4,32,2048]{2,1,0:T(8,128)(2,1)S(1)}, u32[]{:S(2)}, u32[]{:S(2)}) collective-permute-start(bf16[4,32,2048]{2,1,0:T(8,128)(2,1)S(1)} %all-to-all-done.1), channel_id=1, source_target_pairs={{0,2},{1,3},{2,0},{3,1},{4,6},{5,7},{6,4},{7,5},{8,10},{9,11},{10,... | collective-permute-start | bytes 1572872 | tf_op jit(solution)/shard_map/ppermute | solution.py:46
  66.7 21.4 %collective-permute-start.2 = (bf16[4,32,2048]{2,1,0:T(8,128)(2,1)S(1)}, bf16[4,32,2048]{2,1,0:T(8,128)(2,1)S(1)}, u32[]{:S(2)}, u32[]{:S(2)}) collective-permute-start(bf16[4,32,2048]{2,1,0:T(8,128)(2,1)S(1)} %all-to-all-done.1), channel_id=1, source_target_pairs={{0,3},{1,0},{2,1},{3,2},{4,7},{5,4},{6,5},{7,6},{8,11},{9,8},{10,9... | collective-permute-start | bytes 1572872 | tf_op jit(solution)/shard_map/ppermute | solution.py:46
  68.2 21.3 %collective-permute-start.3 = (bf16[4,32,2048]{2,1,0:T(8,128)(2,1)S(1)}, bf16[4,32,2048]{2,1,0:T(8,128)(2,1)S(1)}, u32[]{:S(2)}, u32[]{:S(2)}) collective-permute-start(bf16[4,32,2048]{2,1,0:T(8,128)(2,1)S(1)} %all-to-all-done.1), channel_id=1, source_target_pairs={{0,4},{4,0},{1,5},{5,1},{2,6},{6,2},{3,7},{7,3},{8,12},{12,8},{9,1... | collective-permute-start | bytes 1572872 | tf_op jit(solution)/shard_map/ppermute | solution.py:46
  77.5 12.7 %collective-permute-start.4 = (bf16[4,32,2048]{2,1,0:T(8,128)(2,1)S(1)}, bf16[4,32,2048]{2,1,0:T(8,128)(2,1)S(1)}, u32[]{:S(2)}, u32[]{:S(2)}) collective-permute-start(bf16[4,32,2048]{2,1,0:T(8,128)(2,1)S(1)} %collective-permute-done), channel_id=1, source_target_pairs={{0,4},{4,0},{1,5},{5,1},{2,6},{6,2},{3,7},{7,3},{8,12},{12,8},{9,1... | collective-permute-start | bytes 1572872 | tf_op jit(solution)/shard_map/ppermute | solution.py:46
  101.7 31.7 %collective-permute-start.7 = (bf16[16,2048]{1,0:T(8,128)(2,1)}, bf16[16,2048]{1,0:T(8,128)(2,1)S(1)}, u32[]{:S(2)}, u32[]{:S(2)}) collective-permute-start(bf16[16,2048]{1,0:T(8,128)(2,1)} %get-tuple-element.28), channel_id=1, source_target_pairs={{0,8},{8,16},{16,24},{24,0},{1,9},{9,17},{17,25},{25,1},{2,10},{10... | collective-permute-start | bytes 196616 | tf_op jit(solution)/shard_map/ppermute | solution.py:46
  101.7 32.7 %collective-permute-start.8 = (bf16[16,2048]{1,0:T(8,128)(2,1)S(1)}, bf16[16,2048]{1,0:T(8,128)(2,1)}, u32[]{:S(2)}, u32[]{:S(2)}) collective-permute-start(bf16[16,2048]{1,0:T(8,128)(2,1)S(1)} %get-tuple-element.27), channel_id=1, source_target_pairs={{0,16},{8,24},{16,0},{24,8},{1,17},{9,25},{17,1},{25,9},{2,18},{10... | collective-permute-start | bytes 196616 | tf_op jit(solution)/shard_map/ppermute | solution.py:46
  120.8 13.7 %collective-permute-start.9 = (bf16[16,2048]{1,0:T(8,128)(2,1)S(1)}, bf16[16,2048]{1,0:T(8,128)(2,1)S(1)}, u32[]{:S(2)}, u32[]{:S(2)}) collective-permute-start(bf16[16,2048]{1,0:T(8,128)(2,1)S(1)} %get-tuple-element.29), channel_id=1, source_target_pairs={{0,24},{8,0},{16,8},{24,16},{1,25},{9,1},{17,9},{25,17},{2,26},{10... | collective-permute-start | bytes 196616 | tf_op jit(solution)/shard_map/ppermute | solution.py:46
  121.3 14.3 %collective-permute-start.42 = (bf16[16,2048]{1,0:T(8,128)(2,1)}, bf16[16,2048]{1,0:T(8,128)(2,1)}, u32[]{:S(2)}, u32[]{:S(2)}) collective-permute-start(bf16[16,2048]{1,0:T(8,128)(2,1)} %get-tuple-element.35), channel_id=1, source_target_pairs={{0,8},{8,16},{16,24},{24,0},{1,9},{9,17},{17,25},{25,1},{2,10},{10... | collective-permute-start | bytes 196616 | tf_op jit(solution)/shard_map/ppermute | solution.py:46
  122.8 12.7 %collective-permute-start.43 = (bf16[16,2048]{1,0:T(8,128)(2,1)}, bf16[16,2048]{1,0:T(8,128)(2,1)}, u32[]{:S(2)}, u32[]{:S(2)}) collective-permute-start(bf16[16,2048]{1,0:T(8,128)(2,1)} %get-tuple-element.34), channel_id=1, source_target_pairs={{0,16},{8,24},{16,0},{24,8},{1,17},{9,25},{17,1},{25,9},{2,18},{10... | collective-permute-start | bytes 196616 | tf_op jit(solution)/shard_map/ppermute | solution.py:46
  144.4 18.2 %collective-permute-start.46 = (bf16[64,1280]{1,0:T(8,128)(2,1)S(1)}, bf16[64,1280]{1,0:T(8,128)(2,1)S(1)}, u32[]{:S(2)}, u32[]{:S(2)}) collective-permute-start(bf16[64,1280]{1,0:T(8,128)(2,1)S(1)} %get-tuple-element.48), channel_id=1, source_target_pairs={{0,16},{8,24},{16,0},{24,8},{1,17},{9,25},{17,1},{25,9},{2,18},{10... | collective-permute-start | bytes 491528 | tf_op jit(solution)/shard_map/ppermute | solution.py:46
  146.8 15.8 %collective-permute-start.47 = (bf16[64,1280]{1,0:T(8,128)(2,1)S(1)}, bf16[64,1280]{1,0:T(8,128)(2,1)S(1)}, u32[]{:S(2)}, u32[]{:S(2)}) collective-permute-start(bf16[64,1280]{1,0:T(8,128)(2,1)S(1)} %get-tuple-element.47), channel_id=1, source_target_pairs={{0,24},{8,0},{16,8},{24,16},{1,25},{9,1},{17,9},{25,17},{2,26},{10... | collective-permute-start | bytes 491528 | tf_op jit(solution)/shard_map/ppermute | solution.py:46
  149.7 15.2 %collective-permute-start.10 = (bf16[64,1280]{1,0:T(8,128)(2,1)}, bf16[64,1280]{1,0:T(8,128)(2,1)S(1)}, u32[]{:S(2)}, u32[]{:S(2)}) collective-permute-start(bf16[64,1280]{1,0:T(8,128)(2,1)} %get-tuple-element.43), channel_id=1, source_target_pairs={{0,8},{8,16},{16,24},{24,0},{1,9},{9,17},{17,25},{25,1},{2,10},{10... | collective-permute-start | bytes 491528 | tf_op jit(solution)/shard_map/ppermute | solution.py:46
  151.1 20.4 %collective-permute-start.11 = (bf16[64,1280]{1,0:T(8,128)(2,1)S(1)}, bf16[64,1280]{1,0:T(8,128)(2,1)S(1)}, u32[]{:S(2)}, u32[]{:S(2)}) collective-permute-start(bf16[64,1280]{1,0:T(8,128)(2,1)S(1)} %get-tuple-element.45), channel_id=1, source_target_pairs={{0,16},{8,24},{16,0},{24,8},{1,17},{9,25},{17,1},{25,9},{2,18},{10... | collective-permute-start | bytes 491528 | tf_op jit(solution)/shard_map/ppermute | solution.py:46
  152.3 19.2 %collective-permute-start.12 = (bf16[64,1280]{1,0:T(8,128)(2,1)S(1)}, bf16[64,1280]{1,0:T(8,128)(2,1)S(1)}, u32[]{:S(2)}, u32[]{:S(2)}) collective-permute-start(bf16[64,1280]{1,0:T(8,128)(2,1)S(1)} %get-tuple-element.44), channel_id=1, source_target_pairs={{0,24},{8,0},{16,8},{24,16},{1,25},{9,1},{17,9},{25,17},{2,26},{10... | collective-permute-start | bytes 491528 | tf_op jit(solution)/shard_map/ppermute | solution.py:46
  185.5 11.9 %collective-permute-start.16 = (bf16[16,8192]{1,0:T(8,128)(2,1)S(1)}, bf16[16,8192]{1,0:T(8,128)(2,1)S(1)}, u32[]{:S(2)}, u32[]{:S(2)}) collective-permute-start(bf16[16,8192]{1,0:T(8,128)(2,1)S(1)} %get-tuple-element.23), channel_id=1, source_target_pairs={{0,1},{1,2},{2,3},{3,0},{4,5},{5,6},{6,7},{7,4},{8,9},{9,10},{10,1... | collective-permute-start | bytes 786440 | tf_op jit(solution)/shard_map/ppermute | solution.py:46
  188.2 13.1 %collective-permute-start.17 = (bf16[16,8192]{1,0:T(8,128)(2,1)S(1)}, bf16[16,8192]{1,0:T(8,128)(2,1)S(1)}, u32[]{:S(2)}, u32[]{:S(2)}) collective-permute-start(bf16[16,8192]{1,0:T(8,128)(2,1)S(1)} %get-tuple-element.25), channel_id=1, source_target_pairs={{0,2},{1,3},{2,0},{3,1},{4,6},{5,7},{6,4},{7,5},{8,10},{9,11},{10,... | collective-permute-start | bytes 786440 | tf_op jit(solution)/shard_map/ppermute | solution.py:46
  188.5 13.0 %collective-permute-start.18 = (bf16[16,8192]{1,0:T(8,128)(2,1)S(1)}, bf16[16,8192]{1,0:T(8,128)(2,1)S(1)}, u32[]{:S(2)}, u32[]{:S(2)}) collective-permute-start(bf16[16,8192]{1,0:T(8,128)(2,1)S(1)} %get-tuple-element.24), channel_id=1, source_target_pairs={{0,3},{1,0},{2,1},{3,2},{4,7},{5,4},{6,5},{7,6},{8,11},{9,8},{10,9... | collective-permute-start | bytes 786440 | tf_op jit(solution)/shard_map/ppermute | solution.py:46
  195.2 11.7 %collective-permute-start.51 = (bf16[16,8192]{1,0:T(8,128)(2,1)S(1)}, bf16[16,8192]{1,0:T(8,128)(2,1)S(1)}, u32[]{:S(2)}, u32[]{:S(2)}) collective-permute-start(bf16[16,8192]{1,0:T(8,128)(2,1)S(1)} %get-tuple-element.30), channel_id=1, source_target_pairs={{0,1},{1,2},{2,3},{3,0},{4,5},{5,6},{6,7},{7,4},{8,9},{9,10},{10,1... | collective-permute-start | bytes 786440 | tf_op jit(solution)/shard_map/ppermute | solution.py:46
  195.6 16.0 %collective-permute-start.52 = (bf16[16,8192]{1,0:T(8,128)(2,1)S(1)}, bf16[16,8192]{1,0:T(8,128)(2,1)S(1)}, u32[]{:S(2)}, u32[]{:S(2)}) collective-permute-start(bf16[16,8192]{1,0:T(8,128)(2,1)S(1)} %get-tuple-element.32), channel_id=1, source_target_pairs={{0,2},{1,3},{2,0},{3,1},{4,6},{5,7},{6,4},{7,5},{8,10},{9,11},{10,... | collective-permute-start | bytes 786440 | tf_op jit(solution)/shard_map/ppermute | solution.py:46
  197.4 14.6 %collective-permute-start.53 = (bf16[16,8192]{1,0:T(8,128)(2,1)S(1)}, bf16[16,8192]{1,0:T(8,128)(2,1)S(1)}, u32[]{:S(2)}, u32[]{:S(2)}) collective-permute-start(bf16[16,8192]{1,0:T(8,128)(2,1)S(1)} %get-tuple-element.31), channel_id=1, source_target_pairs={{0,3},{1,0},{2,1},{3,2},{4,7},{5,4},{6,5},{7,6},{8,11},{9,8},{10,9... | collective-permute-start | bytes 786440 | tf_op jit(solution)/shard_map/ppermute | solution.py:46
  212.8 14.8 %collective-permute-start.57 = (bf16[16,2048]{1,0:T(8,128)(2,1)S(1)}, bf16[16,2048]{1,0:T(8,128)(2,1)S(1)}, u32[]{:S(2)}, u32[]{:S(2)}) collective-permute-start(bf16[16,2048]{1,0:T(8,128)(2,1)S(1)} %get-tuple-element.79), channel_id=1, source_target_pairs={{0,8},{8,16},{16,24},{24,0},{1,9},{9,17},{17,25},{25,1},{2,10},{10... | collective-permute-start | bytes 196616 | tf_op jit(solution)/shard_map/ppermute | solution.py:46
  216.7 12.7 %collective-permute-start.58 = (bf16[16,2048]{1,0:T(8,128)(2,1)S(1)}, bf16[16,2048]{1,0:T(8,128)(2,1)S(1)}, u32[]{:S(2)}, u32[]{:S(2)}) collective-permute-start(bf16[16,2048]{1,0:T(8,128)(2,1)S(1)} %get-tuple-element.78), channel_id=1, source_target_pairs={{0,16},{8,24},{16,0},{24,8},{1,17},{9,25},{17,1},{25,9},{2,18},{10... | collective-permute-start | bytes 196616 | tf_op jit(solution)/shard_map/ppermute | solution.py:46
  233.7 17.2 %collective-permute-start.61 = (bf16[4,16,2048]{2,1,0:T(8,128)(2,1)S(1)}, bf16[4,16,2048]{2,1,0:T(8,128)(2,1)}, u32[]{:S(2)}, u32[]{:S(2)}) collective-permute-start(bf16[4,16,2048]{2,1,0:T(8,128)(2,1)S(1)} %get-tuple-element.76), channel_id=1, source_target_pairs={{0,2},{1,3},{2,0},{3,1},{4,6},{5,7},{6,4},{7,5},{8,10},{9,11},{10,... | collective-permute-start | bytes 786440 | tf_op jit(solution)/shard_map/ppermute | solution.py:46
  235.4 16.9 %collective-permute-start.62 = (bf16[4,16,2048]{2,1,0:T(8,128)(2,1)S(1)}, bf16[4,16,2048]{2,1,0:T(8,128)(2,1)}, u32[]{:S(2)}, u32[]{:S(2)}) collective-permute-start(bf16[4,16,2048]{2,1,0:T(8,128)(2,1)S(1)} %get-tuple-element.76), channel_id=1, source_target_pairs={{0,3},{1,0},{2,1},{3,2},{4,7},{5,4},{6,5},{7,6},{8,11},{9,8},{10,9... | collective-permute-start | bytes 786440 | tf_op jit(solution)/shard_map/ppermute | solution.py:46
  239.6 20.7 %collective-permute-start.25 = (bf16[4,16,2048]{2,1,0:T(8,128)(2,1)S(1)}, bf16[4,16,2048]{2,1,0:T(8,128)(2,1)S(1)}, u32[]{:S(2)}, u32[]{:S(2)}) collective-permute-start(bf16[4,16,2048]{2,1,0:T(8,128)(2,1)S(1)} %get-tuple-element.70), channel_id=1, source_target_pairs={{0,1},{1,2},{2,3},{3,0},{4,5},{5,6},{6,7},{7,4},{8,9},{9,10},{10,1... | collective-permute-start | bytes 786440 | tf_op jit(solution)/shard_map/ppermute | solution.py:46
  239.6 21.0 %collective-permute-start.26 = (bf16[4,16,2048]{2,1,0:T(8,128)(2,1)S(1)}, bf16[4,16,2048]{2,1,0:T(8,128)(2,1)}, u32[]{:S(2)}, u32[]{:S(2)}) collective-permute-start(bf16[4,16,2048]{2,1,0:T(8,128)(2,1)S(1)} %get-tuple-element.70), channel_id=1, source_target_pairs={{0,2},{1,3},{2,0},{3,1},{4,6},{5,7},{6,4},{7,5},{8,10},{9,11},{10,... | collective-permute-start | bytes 786440 | tf_op jit(solution)/shard_map/ppermute | solution.py:46
  243.5 17.7 %collective-permute-start.27 = (bf16[4,16,2048]{2,1,0:T(8,128)(2,1)S(1)}, bf16[4,16,2048]{2,1,0:T(8,128)(2,1)S(1)}, u32[]{:S(2)}, u32[]{:S(2)}) collective-permute-start(bf16[4,16,2048]{2,1,0:T(8,128)(2,1)S(1)} %get-tuple-element.70), channel_id=1, source_target_pairs={{0,3},{1,0},{2,1},{3,2},{4,7},{5,4},{6,5},{7,6},{8,11},{9,8},{10,9... | collective-permute-start | bytes 786440 | tf_op jit(solution)/shard_map/ppermute | solution.py:46
  251.0 109.2 %collective-permute-start.41 = (bf16[64,2048]{1,0:T(8,128)(2,1)S(1)}, bf16[64,2048]{1,0:T(8,128)(2,1)}, u32[]{:S(2)}, u32[]{:S(2)}) collective-permute-start(bf16[64,2048]{1,0:T(8,128)(2,1)S(1)} %bitcast.396), channel_id=1, source_target_pairs={{4,0},{5,1},{6,2},{7,3},{12,8},{13,9},{14,10},{15,11},{20,16},{21,... | collective-permute-start | bytes 786440 | tf_op jit(solution)/shard_map/ppermute | solution.py:153
  252.3 108.9 %collective-permute-start.76 = (bf16[64,2048]{1,0:T(8,128)(2,1)S(1)}, bf16[64,2048]{1,0:T(8,128)(2,1)}, u32[]{:S(2)}, u32[]{:S(2)}) collective-permute-start(bf16[64,2048]{1,0:T(8,128)(2,1)S(1)} %bitcast.397), channel_id=1, source_target_pairs={{4,0},{5,1},{6,2},{7,3},{12,8},{13,9},{14,10},{15,11},{20,16},{21,... | collective-permute-start | bytes 786440 | tf_op jit(solution)/shard_map/ppermute | solution.py:153
  260.3 10.4 %collective-permute-start.66 = (f32[64,8]{0,1:T(8,128)S(1)}, f32[64,8]{0,1:T(8,128)S(1)}, u32[]{:S(2)}, u32[]{:S(2)}) collective-permute-start(f32[64,8]{0,1:T(8,128)S(1)} %get-tuple-element.106), channel_id=1, source_target_pairs={{0,8},{8,16},{16,24},{24,0},{1,9},{9,17},{17,25},{25,1},{2,10},{10... | collective-permute-start | bytes 6152 | tf_op jit(solution)/shard_map/ppermute | solution.py:46
  260.7 10.6 %collective-permute-start.67 = (f32[64,8]{0,1:T(8,128)S(1)}, f32[64,8]{0,1:T(8,128)S(1)}, u32[]{:S(2)}, u32[]{:S(2)}) collective-permute-start(f32[64,8]{0,1:T(8,128)S(1)} %get-tuple-element.108), channel_id=1, source_target_pairs={{0,16},{8,24},{16,0},{24,8},{1,17},{9,25},{17,1},{25,9},{2,18},{10... | collective-permute-start | bytes 6152 | tf_op jit(solution)/shard_map/ppermute | solution.py:46
  261.2 11.6 %collective-permute-start.68 = (f32[64,8]{0,1:T(8,128)S(1)}, f32[64,8]{0,1:T(8,128)S(1)}, u32[]{:S(2)}, u32[]{:S(2)}) collective-permute-start(f32[64,8]{0,1:T(8,128)S(1)} %get-tuple-element.107), channel_id=1, source_target_pairs={{0,24},{8,0},{16,8},{24,16},{1,25},{9,1},{17,9},{25,17},{2,26},{10... | collective-permute-start | bytes 6152 | tf_op jit(solution)/shard_map/ppermute | solution.py:46
  278.1 15.6 %collective-permute-start.64 = (bf16[64,1280]{1,0:T(8,128)(2,1)}, bf16[64,1280]{1,0:T(8,128)(2,1)S(1)}, u32[]{:S(2)}, u32[]{:S(2)}) collective-permute-start(bf16[64,1280]{1,0:T(8,128)(2,1)} %get-tuple-element.42), channel_id=1, source_target_pairs={{0,16},{8,24},{16,0},{24,8},{1,17},{9,25},{17,1},{25,9},{2,18},{10... | collective-permute-start | bytes 491528 | tf_op jit(solution)/shard_map/ppermute | solution.py:46
  279.3 14.4 %collective-permute-start.65 = (bf16[64,1280]{1,0:T(8,128)(2,1)S(1)}, bf16[64,1280]{1,0:T(8,128)(2,1)S(1)}, u32[]{:S(2)}, u32[]{:S(2)}) collective-permute-start(bf16[64,1280]{1,0:T(8,128)(2,1)S(1)} %get-tuple-element.41), channel_id=1, source_target_pairs={{0,24},{8,0},{16,8},{24,16},{1,25},{9,1},{17,9},{25,17},{2,26},{10... | collective-permute-start | bytes 491528 | tf_op jit(solution)/shard_map/ppermute | solution.py:46
  287.2 14.1 %collective-permute-start.28 = (bf16[64,1280]{1,0:T(8,128)(2,1)}, bf16[64,1280]{1,0:T(8,128)(2,1)}, u32[]{:S(2)}, u32[]{:S(2)}) collective-permute-start(bf16[64,1280]{1,0:T(8,128)(2,1)} %get-tuple-element.37), channel_id=1, source_target_pairs={{0,8},{8,16},{16,24},{24,0},{1,9},{9,17},{17,25},{25,1},{2,10},{10... | collective-permute-start | bytes 491528 | tf_op jit(solution)/shard_map/ppermute | solution.py:46
  293.7 13.8 %collective-permute-start.29 = (bf16[64,1280]{1,0:T(8,128)(2,1)}, bf16[64,1280]{1,0:T(8,128)(2,1)}, u32[]{:S(2)}, u32[]{:S(2)}) collective-permute-start(bf16[64,1280]{1,0:T(8,128)(2,1)} %get-tuple-element.39), channel_id=1, source_target_pairs={{0,16},{8,24},{16,0},{24,8},{1,17},{9,25},{17,1},{25,9},{2,18},{10... | collective-permute-start | bytes 491528 | tf_op jit(solution)/shard_map/ppermute | solution.py:46
  293.7 16.7 %collective-permute-start.30 = (bf16[64,1280]{1,0:T(8,128)(2,1)}, bf16[64,1280]{1,0:T(8,128)(2,1)}, u32[]{:S(2)}, u32[]{:S(2)}) collective-permute-start(bf16[64,1280]{1,0:T(8,128)(2,1)} %get-tuple-element.38), channel_id=1, source_target_pairs={{0,24},{8,0},{16,8},{24,16},{1,25},{9,1},{17,9},{25,17},{2,26},{10... | collective-permute-start | bytes 491528 | tf_op jit(solution)/shard_map/ppermute | solution.py:46
  321.5 14.0 %collective-permute-start.35 = (bf16[16,8192]{1,0:T(8,128)(2,1)S(1)}, bf16[16,8192]{1,0:T(8,128)(2,1)S(1)}, u32[]{:S(2)}, u32[]{:S(2)}) collective-permute-start(bf16[16,8192]{1,0:T(8,128)(2,1)S(1)} %get-tuple-element.19), channel_id=1, source_target_pairs={{0,2},{1,3},{2,0},{3,1},{4,6},{5,7},{6,4},{7,5},{8,10},{9,11},{10,... | collective-permute-start | bytes 786440 | tf_op jit(solution)/shard_map/ppermute | solution.py:46
  321.6 14.0 %collective-permute-start.36 = (bf16[16,8192]{1,0:T(8,128)(2,1)S(1)}, bf16[16,8192]{1,0:T(8,128)(2,1)S(1)}, u32[]{:S(2)}, u32[]{:S(2)}) collective-permute-start(bf16[16,8192]{1,0:T(8,128)(2,1)S(1)} %get-tuple-element.18), channel_id=1, source_target_pairs={{0,3},{1,0},{2,1},{3,2},{4,7},{5,4},{6,5},{7,6},{8,11},{9,8},{10,9... | collective-permute-start | bytes 786440 | tf_op jit(solution)/shard_map/ppermute | solution.py:46
  331.6 11.3 %collective-permute-start.69 = (bf16[16,8192]{1,0:T(8,128)(2,1)S(1)}, bf16[16,8192]{1,0:T(8,128)(2,1)S(1)}, u32[]{:S(2)}, u32[]{:S(2)}) collective-permute-start(bf16[16,8192]{1,0:T(8,128)(2,1)S(1)} %get-tuple-element.20), channel_id=1, source_target_pairs={{0,1},{1,2},{2,3},{3,0},{4,5},{5,6},{6,7},{7,4},{8,9},{9,10},{10,1... | collective-permute-start | bytes 786440 | tf_op jit(solution)/shard_map/ppermute | solution.py:46
  335.6 12.8 %collective-permute-start.70 = (bf16[16,8192]{1,0:T(8,128)(2,1)S(1)}, bf16[16,8192]{1,0:T(8,128)(2,1)S(1)}, u32[]{:S(2)}, u32[]{:S(2)}) collective-permute-start(bf16[16,8192]{1,0:T(8,128)(2,1)S(1)} %get-tuple-element.22), channel_id=1, source_target_pairs={{0,2},{1,3},{2,0},{3,1},{4,6},{5,7},{6,4},{7,5},{8,10},{9,11},{10,... | collective-permute-start | bytes 786440 | tf_op jit(solution)/shard_map/ppermute | solution.py:46
  335.6 12.8 %collective-permute-start.71 = (bf16[16,8192]{1,0:T(8,128)(2,1)S(1)}, bf16[16,8192]{1,0:T(8,128)(2,1)S(1)}, u32[]{:S(2)}, u32[]{:S(2)}) collective-permute-start(bf16[16,8192]{1,0:T(8,128)(2,1)S(1)} %get-tuple-element.21), channel_id=1, source_target_pairs={{0,3},{1,0},{2,1},{3,2},{4,7},{5,4},{6,5},{7,6},{8,11},{9,8},{10,9... | collective-permute-start | bytes 786440 | tf_op jit(solution)/shard_map/ppermute | solution.py:46
  (54 other events, 564.9 us)
Sparse Core Ops, SparseCore 0:
  10.7 20.4 all-reduce.2
  32.7 23.9 all-gather.8
  58.3 33.2 all-gather.10
